TPU v7x, 128 devices: a whole 4x4x4 slice. The times are simulated.
128 devices in a mesh: shot: 2 (over core), strip: 64 (over z, y, x).
Axes of the slice: x: 4, y: 4, z: 4, core: 2. Of those that a mesh axis runs over, the one named last changes fastest.
Arguments:
- source_now: float32 [2, 64, 2048, 256], P('shot', None, 'strip'), may hold values from -8 to 8
- source_prev: float32 [2, 64, 2048, 256], P('shot', None, 'strip'), may hold values from -8 to 8
- adjoint_now: float32 [2, 64, 2048, 256], P('shot', None, 'strip'), may hold values from -8 to 8
- adjoint_prev: float32 [2, 64, 2048, 256], P('shot', None, 'strip'), may hold values from -8 to 8
- courant: float32 [2048, 256], P('strip'), may hold values from 0.08 to 0.45
- probe_left: float32 [16, 2048, 256], P(None, 'strip'), may hold values from -6 to 6
- probe_right: float32 [16, 2048, 256], P(None, 'strip'), may hold values from -6 to 6
Outputs:
- left_factor: float32 [16, 2048, 256], P(None, 'strip')
- right_factor: float32 [16, 2048, 256], P(None, 'strip')
All inputs are finite; a program needn't handle non-finite values.
Results may differ from a plain program's by a relative error of at most 0.0003.
Values sent between devices are 32-bit elements; how exact they have to be, the bound alone decides.
A program may use at most 64 MiB of HBM per device.

v0:
```python
import math

import jax
import jax.numpy as jnp
from jax import lax
from jax.sharding import PartitionSpec as P

STEPS = 8


def extended(cells, sides, width):
    for axis, dim in sides:
        count = lax.axis_size(axis)
        ends = count - 1
        head = lax.slice_in_dim(cells, 0, width, axis=dim)
        tail = lax.slice_in_dim(cells, cells.shape[dim] - width, cells.shape[dim], axis=dim)
        cells = jnp.concatenate(
            [
                lax.ppermute(tail, axis, [(i, (i + 1) % count) for i in range(ends)]),
                cells,
                lax.ppermute(head, axis, [((i + 1) % count, i) for i in range(ends)]),
            ],
            axis=dim,
        )
    return cells


def sideways(fields):
    zero_column = jnp.zeros_like(fields[..., :1])
    return jnp.concatenate([fields[..., 1:], zero_column], -1) + jnp.concatenate(
        [zero_column, fields[..., :-1]], -1
    )


def advance(centre, before, above_below, speed_local):
    laplace = above_below + sideways(centre) - 4.0 * centre
    return 2.0 * centre - before + speed_local[None] * laplace


def gram_matrix(sketch):
    flattened = sketch.reshape(sketch.shape[0], -1)
    return jnp.dot(flattened, flattened.T, precision=lax.Precision.HIGHEST)


def orthonormal(sketch, gram_value, factor_scale):
    lower_factor = jnp.linalg.cholesky(gram_value)
    flattened = sketch.reshape(sketch.shape[0], -1)
    solved = lax.linalg.triangular_solve(lower_factor, flattened, left_side=True, lower=True)
    return (solved * factor_scale).reshape(sketch.shape)


def shards(source_now, source_prev, adjoint_now, adjoint_prev, courant, probe_left, probe_right):
    wave_count = source_now.shape[1]
    field_now = jnp.concatenate([source_now[0], adjoint_now[0]], 0)
    field_prev = jnp.concatenate([source_prev[0], adjoint_prev[0]], 0)
    row_count = field_now.shape[1]
    for step_index in range(STEPS):
        padded = extended(field_now, (("strip", 1),), 1)
        field_next = advance(field_now, field_prev, padded[:, 2:] + padded[:, :-2], courant)
        field_prev, field_now = (field_now, field_next)
    rank_count = probe_left.shape[0]
    flat_source = field_now[:wave_count].reshape(wave_count, -1)
    flat_adjoint = field_now[wave_count:].reshape(wave_count, -1)
    left_probe = jnp.dot(
        flat_adjoint, probe_left.reshape(rank_count, -1).T, precision=lax.Precision.HIGHEST
    )
    right_probe = jnp.dot(
        flat_source, probe_right.reshape(rank_count, -1).T, precision=lax.Precision.HIGHEST
    )
    left_probe, right_probe = lax.psum((left_probe, right_probe), "strip")
    left_local = jnp.dot(left_probe.T, flat_source, precision=lax.Precision.HIGHEST).reshape(
        rank_count, row_count, -1
    )
    right_local = jnp.dot(right_probe.T, flat_adjoint, precision=lax.Precision.HIGHEST).reshape(
        rank_count, row_count, -1
    )
    factor_scale = math.sqrt(row_count * lax.axis_size("strip") * left_local.shape[2])
    left_sum, right_sum = lax.psum((left_local, right_local), "shot")
    gram_pair = lax.psum((gram_matrix(left_sum), gram_matrix(right_sum)), "strip")
    left_factor = orthonormal(left_sum, gram_pair[0], factor_scale)
    right_factor = orthonormal(right_sum, gram_pair[1], factor_scale)
    return (left_factor, right_factor)


def solution(mesh):
    return jax.shard_map(
        shards,
        mesh=mesh,
        in_specs=(
            P("shot", None, "strip", None),
            P("shot", None, "strip", None),
            P("shot", None, "strip", None),
            P("shot", None, "strip", None),
            P("strip", None),
            P(None, "strip", None),
            P(None, "strip", None),
        ),
        out_specs=(P(None, "strip", None), P(None, "strip", None)),
        check_vma=False,
    )
```

profile of v0, /device:TPU:0, one launch (start us, length us, event | category | flops | bytes accessed | tf_op | source)
XLA Modules:
  0.0 892.7 jit_solution(14271612222504190252)
XLA Ops:
  7.2 1.9 fusion.60
  9.1 1.4 collective-permute-start
  10.6 4.7 collective-permute-start.1
  15.3 4.3 fusion
  19.6 8.1 fusion.41
  27.9 1.3 collective-permute-start.2
  29.2 4.6 collective-permute-start.3
  33.7 3.4 fusion.83
  37.1 6.1 fusion.36
  43.5 1.3 collective-permute-start.4
  44.8 4.6 collective-permute-start.5
  49.3 1.7 fusion.81
  51.8 3.6 fusion.31
  55.6 1.3 collective-permute-start.6
  56.9 5.2 collective-permute-start.7
  62.1 1.7 fusion.79
  64.4 3.6 fusion.26
  68.1 1.3 collective-permute-start.8
  69.4 6.6 collective-permute-start.9
  76.0 1.7 fusion.77
  78.5 3.6 fusion.21
  82.3 1.3 collective-permute-start.10
  83.6 6.7 collective-permute-start.11
  90.3 1.7 fusion.75
  92.8 3.6 fusion.16
  96.5 1.3 collective-permute-start.12
  97.8 7.3 collective-permute-start.13
  105.2 1.7 fusion.73
  107.4 3.6 fusion.11
  111.2 1.3 collective-permute-start.14
  112.5 7.1 collective-permute-start.15
  119.6 1.7 fusion.71
  122.1 3.6 fusion.6
  125.7 1.7 fusion.70
  127.4 4.6 fusion.52
  131.9 3.1 fusion.55
  135.0 358.9 %all-reduce.17 = (f32[64,16]{0,1:T(8,128)S(1)}, f32[64,16]{0,1:T(8,128)S(1)}) all-reduce(f32[64,16]{0,1:T(8,128)S(1)} %fusion.52, f32[64,16]{0,1:T(8,128)S(1)} %fusion.55), channel_id=1, replica_groups=mesh['shot'=2,'strip'=64] {'strip'}, use_global_device_ids=true, to_apply=%region_0.0 | all-reduce | flops 2048 | bytes 16384 | tf_op jit(solution)/shard_map/psum | solution.py:70
  493.9 4.6 fusion.42
  498.4 3.0 fusion.45
  501.5 18.6 %all-reduce.21.cloned.1.call-done = (f32[16,32,256]{2,0,1:T(8,128)}, f32[16,32,256]{2,0,1:T(8,128)}) async-done(((f32[16,32,256]{2,0,1:T(8,128)}, f32[16,32,256]{2,0,1:T(8,128)}), (f32[16,32,256]{2,0,1:T(8,128)}, f32[16,32,256]{2,0,1:T(8,128)})) %all-reduce.21.cloned.1.call-update) | async-done | bytes 1048592 | tf_op jit(solution)/shard_map/psum | solution.py:78
  520.1 2.1 convolution_bitcast_fusion.1
  522.1 2.0 convolution_bitcast_fusion
  524.1 348.8 %all-reduce.16 = (f32[16,16]{0,1:T(8,128)S(1)}, f32[16,16]{0,1:T(8,128)S(1)}) all-reduce(f32[16,16]{0,1:T(8,128)S(1)} %convolution_bitcast_fusion.1, f32[16,16]{0,1:T(8,128)S(1)} %convolution_bitcast_fusion), channel_id=1, replica_groups=mesh['shot'=2,'strip'=64] {'strip'}, use_global_device_ids=true, to_apply=%region_2.0 | all-reduce | flops 512 | bytes 4096 | tf_op jit(solution)/shard_map/psum | solution.py:79
  873.1 1.5 cholesky.55
  875.9 1.2 custom-call.7
  877.1 1.5 cholesky.44
  879.9 1.2 custom-call.6
  881.2 1.1 copy.32
  (53 shorter events, 11.9 us)
Async XLA Ops:
  7.2 120.2 %copy-start = (f32[16,32,256]{2,1,0:T(8,128)S(1)}, f32[16,32,256]{2,1,0:T(8,128)}, u32[]{:S(2)}) copy-start(f32[16,32,256]{2,1,0:T(8,128)} %param.15) | copy-start | bytes 1572868
  7.2 8.1 copy-start.1
  7.2 512.9 %all-reduce.21.cloned.1.call-start = ((), (), s32[]{:S(2)}) async-start(), calls=%async_computation | async-start | bytes 2097152 | tf_op jit(solution)/shard_map/psum | solution.py:78
  7.2 8.0 copy-start.2
  9.1 10.5 %collective-permute-start = (f32[128,1,256]{2,1,0:T(1,128)S(1)}, f32[128,1,256]{2,1,0:T(1,128)S(1)}, u32[]{:S(2)}, u32[]{:S(2)}) collective-permute-start(f32[128,1,256]{2,1,0:T(1,128)S(1)} %get-tuple-element.42), channel_id=1, source_target_pairs={{1,0},{2,1},{3,2},{4,3},{5,4},{6,5},{7,6},{8,7},{9,8},{10,9},{11,1... | collective-permute-start | bytes 393224 | tf_op jit(solution)/shard_map/ppermute | solution.py:21
  10.5 9.0 %copy-start.4 = (f32[32,256]{1,0:T(8,128)S(1)}, f32[32,256]{1,0:T(8,128)}, u32[]{:S(2)}) copy-start(f32[32,256]{1,0:T(8,128)} %param.14) | copy-start | bytes 98308
  10.6 9.0 %copy-start.5 = (f32[1,64,32,256]{3,2,1,0:T(8,128)S(1)}, f32[1,64,32,256]{3,2,1,0:T(8,128)}, u32[]{:S(2)}) copy-start(f32[1,64,32,256]{3,2,1,0:T(8,128)} %param.13) | copy-start | bytes 6291460
  10.6 9.0 %collective-permute-start.1 = (f32[128,1,256]{2,1,0:T(1,128)S(1)}, f32[128,1,256]{2,1,0:T(1,128)S(1)}, u32[]{:S(2)}, u32[]{:S(2)}) collective-permute-start(f32[128,1,256]{2,1,0:T(1,128)S(1)} %get-tuple-element.43), channel_id=1, source_target_pairs={{0,1},{1,2},{2,3},{3,4},{4,5},{5,6},{6,7},{7,8},{8,9},{9,10},{10,1... | collective-permute-start | bytes 393224 | tf_op jit(solution)/shard_map/ppermute | solution.py:19
  27.9 9.2 %collective-permute-start.2 = (f32[128,1,256]{2,1,0:T(1,128)S(1)}, f32[128,1,256]{2,1,0:T(1,128)S(1)}, u32[]{:S(2)}, u32[]{:S(2)}) collective-permute-start(f32[128,1,256]{2,1,0:T(1,128)S(1)} %get-tuple-element.38), channel_id=1, source_target_pairs={{1,0},{2,1},{3,2},{4,3},{5,4},{6,5},{7,6},{8,7},{9,8},{10,9},{11,1... | collective-permute-start | bytes 393224 | tf_op jit(solution)/shard_map/ppermute | solution.py:21
  29.2 8.0 collective-permute-start.3
  43.5 7.5 collective-permute-start.4
  44.8 7.1 collective-permute-start.5
  55.6 8.1 collective-permute-start.6
  56.9 7.5 collective-permute-start.7
  68.1 9.6 %collective-permute-start.8 = (f32[128,1,256]{2,1,0:T(1,128)S(1)}, f32[128,1,256]{2,1,0:T(1,128)S(1)}, u32[]{:S(2)}, u32[]{:S(2)}) collective-permute-start(f32[128,1,256]{2,1,0:T(1,128)S(1)} %get-tuple-element.26), channel_id=1, source_target_pairs={{1,0},{2,1},{3,2},{4,3},{5,4},{6,5},{7,6},{8,7},{9,8},{10,9},{11,1... | collective-permute-start | bytes 393224 | tf_op jit(solution)/shard_map/ppermute | solution.py:21
  69.4 9.1 %collective-permute-start.9 = (f32[128,1,256]{2,1,0:T(1,128)S(1)}, f32[128,1,256]{2,1,0:T(1,128)S(1)}, u32[]{:S(2)}, u32[]{:S(2)}) collective-permute-start(f32[128,1,256]{2,1,0:T(1,128)S(1)} %get-tuple-element.27), channel_id=1, source_target_pairs={{0,1},{1,2},{2,3},{3,4},{4,5},{5,6},{6,7},{7,8},{8,9},{9,10},{10,1... | collective-permute-start | bytes 393224 | tf_op jit(solution)/shard_map/ppermute | solution.py:19
  82.3 9.6 %collective-permute-start.10 = (f32[128,1,256]{2,1,0:T(1,128)S(1)}, f32[128,1,256]{2,1,0:T(1,128)S(1)}, u32[]{:S(2)}, u32[]{:S(2)}) collective-permute-start(f32[128,1,256]{2,1,0:T(1,128)S(1)} %get-tuple-element.22), channel_id=1, source_target_pairs={{1,0},{2,1},{3,2},{4,3},{5,4},{6,5},{7,6},{8,7},{9,8},{10,9},{11,1... | collective-permute-start | bytes 393224 | tf_op jit(solution)/shard_map/ppermute | solution.py:21
  83.6 9.2 %collective-permute-start.11 = (f32[128,1,256]{2,1,0:T(1,128)S(1)}, f32[128,1,256]{2,1,0:T(1,128)S(1)}, u32[]{:S(2)}, u32[]{:S(2)}) collective-permute-start(f32[128,1,256]{2,1,0:T(1,128)S(1)} %get-tuple-element.23), channel_id=1, source_target_pairs={{0,1},{1,2},{2,3},{3,4},{4,5},{5,6},{6,7},{7,8},{8,9},{9,10},{10,1... | collective-permute-start | bytes 393224 | tf_op jit(solution)/shard_map/ppermute | solution.py:19
  96.5 10.3 %collective-permute-start.12 = (f32[128,1,256]{2,1,0:T(1,128)S(1)}, f32[128,1,256]{2,1,0:T(1,128)S(1)}, u32[]{:S(2)}, u32[]{:S(2)}) collective-permute-start(f32[128,1,256]{2,1,0:T(1,128)S(1)} %get-tuple-element.18), channel_id=1, source_target_pairs={{1,0},{2,1},{3,2},{4,3},{5,4},{6,5},{7,6},{8,7},{9,8},{10,9},{11,1... | collective-permute-start | bytes 393224 | tf_op jit(solution)/shard_map/ppermute | solution.py:21
  97.8 9.6 %collective-permute-start.13 = (f32[128,1,256]{2,1,0:T(1,128)S(1)}, f32[128,1,256]{2,1,0:T(1,128)S(1)}, u32[]{:S(2)}, u32[]{:S(2)}) collective-permute-start(f32[128,1,256]{2,1,0:T(1,128)S(1)} %get-tuple-element.19), channel_id=1, source_target_pairs={{0,1},{1,2},{2,3},{3,4},{4,5},{5,6},{6,7},{7,8},{8,9},{9,10},{10,1... | collective-permute-start | bytes 393224 | tf_op jit(solution)/shard_map/ppermute | solution.py:19
  111.2 10.1 %collective-permute-start.14 = (f32[128,1,256]{2,1,0:T(1,128)S(1)}, f32[128,1,256]{2,1,0:T(1,128)S(1)}, u32[]{:S(2)}, u32[]{:S(2)}) collective-permute-start(f32[128,1,256]{2,1,0:T(1,128)S(1)} %get-tuple-element.14), channel_id=1, source_target_pairs={{1,0},{2,1},{3,2},{4,3},{5,4},{6,5},{7,6},{8,7},{9,8},{10,9},{11,1... | collective-permute-start | bytes 393224 | tf_op jit(solution)/shard_map/ppermute | solution.py:21
  112.5 9.6 %collective-permute-start.15 = (f32[128,1,256]{2,1,0:T(1,128)S(1)}, f32[128,1,256]{2,1,0:T(1,128)S(1)}, u32[]{:S(2)}, u32[]{:S(2)}) collective-permute-start(f32[128,1,256]{2,1,0:T(1,128)S(1)} %get-tuple-element.15), channel_id=1, source_target_pairs={{0,1},{1,2},{2,3},{3,4},{4,5},{5,6},{6,7},{7,8},{8,9},{9,10},{10,1... | collective-permute-start | bytes 393224 | tf_op jit(solution)/shard_map/ppermute | solution.py:19
  125.7 6.2 copy-start.6
  520.1 363.8 %copy-start.3 = (f32[16,32,256]{2,0,1:T(8,128)S(1)}, f32[16,32,256]{2,0,1:T(8,128)}, u32[]{:S(2)}) copy-start(f32[16,32,256]{2,0,1:T(8,128)} %get-tuple-element.8) | copy-start | bytes 1572868
Sparse Core Ops, SparseCore 0:
  501.6 18.4 all-reduce.20
where the time goes:
time: 902 us; the launch traced here: 893 us
  blocking collectives  708 us (78%)
  starting transfers between devices  57.1 us (6%)
  other arithmetic  49.8 us (6%)
  waiting for transfers between devices  23.1 us (3%)
  matrix products  20.5 us (2%)
  local copies, waits for them, and re-layouts  19.5 us (2%)
  between operations  14.9 us (2%)
    psum x1, blocking collectives, shards(): left_probe, right_probe = lax.psum((left_probe, right_probe), 'strip')  359 us
    psum x1, blocking collectives, shards(): lax.psum((gram_matrix(left_sum), gram_matrix(right_sum)), 'strip')  349 us
    ppermute x8, starting transfers between devices, extended(): lax.ppermute(tail, axis, [(i, (i + 1) % count) for i in range(ends)])  46.6 us
    add x8, other arithmetic, advance(): return 2.0 * centre - before + speed_local[None] * laplace  35.6 us
    psum x1, waiting for transfers between devices, shards(): left_sum, right_sum = lax.psum((left_local, right_local), 'shot')  18.6 us
  transfers between devices with their start and end apart: 17, of which 7 were waited for; matrix products, arithmetic and copies ran while one was open for 2% of the time, Pallas kernels for 0%

commit v1 on v0

v1 whole, which is shorter than its diff:
```python
import functools
import math

import jax
import jax.numpy as jnp
from jax import lax
from jax.experimental import pallas as pl
from jax.experimental.pallas import tpu as pltpu
from jax.sharding import PartitionSpec as P

STEPS = 8
WAVES = 64
RANK = 16
ROWS = 32
COLS = 256
HALF = 128
TALL = ROWS + 2 * STEPS
SIDE = 4
PLANE = SIDE * SIDE
MESH = pl.DeviceIdType.MESH
F32 = jnp.float32
BF16 = jnp.bfloat16


def split(x):
    high = x.astype(BF16)
    low = (x - high.astype(F32)).astype(BF16)
    return high, low


def stacked(x):
    return jnp.concatenate(split(x), 0)


def dot_rows(a, b):
    return lax.dot_general(a, b, (((1,), (1,)), ((), ())), preferred_element_type=F32)


def dot(a, b):
    return lax.dot_general(a, b, (((1,), (0,)), ((), ())), preferred_element_type=F32)


def sideways(x):
    lane = lax.broadcasted_iota(jnp.int32, (RANK, HALF), 1)
    first, second = x[:, :HALF], x[:, HALF:]
    ahead0, ahead1 = pltpu.roll(first, 1, 1), pltpu.roll(second, 1, 1)
    back0, back1 = pltpu.roll(first, HALF - 1, 1), pltpu.roll(second, HALF - 1, 1)
    start, end = lane == 0, lane == HALF - 1
    out0 = jnp.where(start, 0.0, ahead0) + jnp.where(end, back1, back0)
    out1 = jnp.where(start, ahead0, ahead1) + jnp.where(end, 0.0, back1)
    return jnp.concatenate([out0, out1], 1)


def twice(x):
    return jnp.concatenate([x, x], 0)


def sweep(buf, speed, middle, level, low, pairs, transposed):
    now = buf.at[lax.rem(level + 1, 2)]
    new = buf.at[lax.rem(level, 2)]

    def term(r):
        if transposed:
            return twice(speed[r]) * now[r]
        return now[r]

    def put(r, above, centre, below):
        spread = above + below + sideways(centre)
        if not transposed:
            spread = twice(speed[r]) * spread
        new[r] = twice(middle[r]) * now[r] - new[r] + spread

    def body(i, carry):
        above, centre = carry
        r = low + 2 * i
        below = term(r + 1)
        put(r, above, centre, below)
        beyond = term(r + 2)
        put(r + 1, centre, below, beyond)
        return below, beyond

    lax.fori_loop(0, pairs, body, (term(low - 1), term(low)))


def inner_sweeps(buf, speed, middle, transposed):
    def body(level, carry):
        sweep(buf, speed, middle, level, STEPS + level, ROWS // 2 - level, transposed)
        return carry

    lax.fori_loop(1, STEPS + 1, body, 0)


def edge_sweeps(buf, speed, middle, transposed):
    def body(level, carry):
        sweep(buf, speed, middle, level, level, STEPS // 2, transposed)
        sweep(buf, speed, middle, level, STEPS + ROWS - level, STEPS // 2, transposed)
        return carry

    lax.fori_loop(1, STEPS + 1, body, 0)


def lower_inverse(gram):
    row = lax.broadcasted_iota(jnp.int32, (RANK, HALF), 0)
    lane = lax.broadcasted_iota(jnp.int32, (RANK, HALF), 1)
    work = jnp.where(lane < RANK, gram, jnp.where(lane == row + RANK, 1.0, 0.0))
    for k in range(RANK):
        pivot = work[k : k + 1, k : k + 1]
        root = 1.0 / jnp.sqrt(pivot)
        line = work[k : k + 1, :] * root
        column = jnp.where(row[:, :1] > k, work[:, k : k + 1] * root, 0.0)
        work = jnp.where(row == k, line, work - column * line)
    return work


def main_kernel(
    src_now, src_prev, adj_now, adj_prev, courant, left3, right3, left2, right2,
    s_out, inv_out,
    waves, slabs, probes, probe_edges, speed_own, speed_edges, speed, middle,
    steps_p, weights, plane_send, plane_recv, column_send, column_recv, other_gram,
    fields, partial, arrived,
    load_sem, edge_send, edge_recv, sum_send, sum_recv, core_send, core_recv, halo_send, halo_recv, out_sem,
):
    own = lax.axis_index("shot")
    me = lax.axis_index("strip")
    count = lax.axis_size("strip")
    x, y, z = me % SIDE, (me // SIDE) % SIDE, me // PLANE
    after, before = (me + 1) % count, (me + count - 1) % count
    lane = lax.broadcasted_iota(jnp.int32, (RANK, HALF), 1)

    def plane_peer(d):
        return z * PLANE + ((y + d // SIDE) % SIDE) * SIDE + (x + d % SIDE) % SIDE

    def column_peer(d):
        return ((z + d) % SIDE) * PLANE + y * SIDE + x

    def remote(src, dst, send, recv, device):
        return pltpu.make_async_remote_copy(
            src_ref=src, dst_ref=dst, send_sem=send, recv_sem=recv, device_id=device, device_id_type=MESH
        )

    barrier = pltpu.get_barrier_semaphore()
    strips = [plane_peer(d) for d in range(1, PLANE)] + [column_peer(d) for d in range(1, SIDE)] + [after, before]
    for peer in strips:
        pl.semaphore_signal(barrier, inc=1, device_id={"strip": peer}, device_id_type=MESH)
    pl.semaphore_signal(barrier, inc=1, device_id={"shot": 1 - own}, device_id_type=MESH)

    halves = [pl.ds(0, HALF), pl.ds(HALF, HALF)]
    loads = [pltpu.make_async_copy(courant, speed_own, load_sem.at[0])]
    for k, probe in enumerate((left2, right2)):
        for h in range(2):
            loads.append(pltpu.make_async_copy(probe.at[:, halves[h]], probes.at[k, h], load_sem.at[1 + 2 * k + h]))
    for a, wave in enumerate((src_now, src_prev, adj_now, adj_prev)):
        for h in range(2):
            loads.append(pltpu.make_async_copy(wave.at[:, halves[h]], waves.at[a, h], load_sem.at[5 + 2 * a + h]))
    for load in loads:
        load.start()

    pl.semaphore_wait(barrier, len(strips) + 1)

    edges = []
    for side, (target, first) in enumerate(((after, ROWS - STEPS), (before, 0))):
        edges.append(
            remote(courant.at[pl.ds(first, STEPS)], speed_edges.at[side],
                   edge_send.at[side, 0], edge_recv.at[side, 0], {"strip": target})
        )
    for k, probe in enumerate((left3, right3)):
        for side, (target, first) in enumerate(((after, ROWS - STEPS), (before, 0))):
            for h in range(2):
                at = 1 + 2 * k + h
                edges.append(
                    remote(probe.at[:, pl.ds(first, STEPS), halves[h]], probe_edges.at[side, k, h],
                           edge_send.at[side, at], edge_recv.at[side, at], {"strip": target})
                )
    for copy in edges:
        copy.start()

    def put_speed(values, row0):
        for r in range(STEPS):
            value = jnp.broadcast_to(values[r : r + 1, :], (8, COLS))
            speed[row0 + r] = value
            middle[row0 + r] = 2.0 - 4.0 * value

    loads[0].wait()
    for block in range(ROWS // STEPS):
        put_speed(speed_own[pl.ds(block * STEPS, STEPS), :], STEPS + block * STEPS)
    for load in loads[1:5]:
        load.wait()

    def put_probe(r, carry):
        for k in range(2):
            steps_p[k, 0, STEPS + r] = jnp.concatenate(
                [probes[k, h, pl.ds(r, RANK, stride=ROWS), :] for h in range(2)], 1
            )
        return carry

    lax.fori_loop(0, ROWS, put_probe, 0)

    def put_zero(r, carry):
        for k in range(2):
            steps_p[k, 1, r] = jnp.zeros((RANK, COLS), F32)
        return carry

    lax.fori_loop(0, TALL, put_zero, 0)

    for k in range(2):
        inner_sweeps(steps_p.at[k], speed, middle, True)

    for a in range(4):
        loads[5 + 2 * a].wait()
        loads[6 + 2 * a].wait()

        def put_slab(r, carry):
            value = jnp.concatenate([waves[a, h, pl.ds(r, WAVES, stride=ROWS), :] for h in range(2)], 1)
            slabs[a, r] = stacked(value)
            return carry

        lax.fori_loop(0, ROWS, put_slab, 0)

    def products(r, totals):
        out = []
        for k in range(2):
            total = totals[k]
            a = 2 - 2 * k
            total = total + dot_rows(stacked(steps_p[k, 0, STEPS + r]), slabs[a, r])
            total = total - dot_rows(stacked(steps_p[k, 1, STEPS + r]), slabs[a + 1, r])
            out.append(total)
        return tuple(out)

    zero = jnp.zeros((2 * RANK, HALF), F32)
    totals = lax.fori_loop(STEPS, ROWS - STEPS, products, (zero, zero))

    for copy in edges:
        copy.wait_recv()
    inside = (me > 0, me < count - 1)
    for side, row0 in enumerate((0, STEPS + ROWS)):
        put_speed(jnp.where(inside[side], speed_edges[side], 0.0), row0)
        for k in range(2):
            for r in range(STEPS):
                steps_p[k, 0, row0 + r] = jnp.concatenate(
                    [probe_edges.at[side, k, h].reshape(RANK * STEPS, HALF)[pl.ds(r, RANK, stride=STEPS), :] for h in range(2)], 1
                )
    for k in range(2):
        edge_sweeps(steps_p.at[k], speed, middle, True)
    totals = lax.fori_loop(0, STEPS, products, totals)
    totals = lax.fori_loop(ROWS - STEPS, ROWS, products, totals)

    def strip_sum(value, i):
        plane_send[i] = value
        copies = [
            remote(plane_send.at[i], plane_recv.at[i, d - 1], sum_send.at[i, d - 1], sum_recv.at[i, d - 1],
                   {"strip": plane_peer(d)})
            for d in range(1, PLANE)
        ]
        for copy in copies:
            copy.start()
        for d, copy in enumerate(copies):
            copy.wait_recv()
            value = value + plane_recv[i, d]
        column_send[i] = value
        more = [
            remote(column_send.at[i], column_recv.at[i, d - 1], sum_send.at[i, PLANE + d - 2],
                   sum_recv.at[i, PLANE + d - 2], {"strip": column_peer(d)})
            for d in range(1, SIDE)
        ]
        for copy in more:
            copy.start()
        for d, copy in enumerate(more):
            copy.wait_recv()
            value = value + column_recv[i, d]
        for copy in copies + more:
            copy.wait_send()
        return value

    folded = []
    for k in range(2):
        both = totals[k][:RANK] + totals[k][RANK:]
        folded.append(both + pltpu.roll(both, WAVES, 1))
    weight = strip_sum(jnp.where(lane < WAVES, folded[0], folded[1]), 0)
    turned = pltpu.roll(weight, WAVES, 1)
    weights[0] = stacked(jnp.where(lane < WAVES, weight, turned))
    weights[1] = stacked(jnp.where(lane < WAVES, turned, weight))

    def combine(side, level, r):
        both = dot(weights[side], slabs[2 * side + level, r])
        return both[:RANK] + both[RANK:]

    away = 1 - own

    def for_other(r, carry):
        for level in range(2):
            partial[level, r] = combine(away, level, r)
        return carry

    def for_own(r, carry):
        for level in range(2):
            fields[level, STEPS + r] = combine(own, level, r)
        return carry

    def add_arrived(r, carry):
        for level in range(2):
            fields[level, STEPS + r] = fields[level, STEPS + r] + arrived[level, r]
        return carry

    spans = ((0, STEPS), (ROWS - STEPS, ROWS), (STEPS, ROWS - STEPS))

    def core_copies(index):
        lo, hi = spans[index]
        return [
            remote(partial.at[level, pl.ds(lo, hi - lo)], arrived.at[level, pl.ds(lo, hi - lo)],
                   core_send.at[2 * index + level], core_recv.at[2 * index + level], {"shot": away})
            for level in range(2)
        ]

    crossing = []
    for index in range(2):
        lax.fori_loop(*spans[index], for_other, 0)
        copies = core_copies(index)
        for copy in copies:
            copy.start()
        crossing.append(copies)
    halos = []
    for index in range(2):
        lax.fori_loop(*spans[index], for_own, 0)
    for index in range(2):
        for copy in crossing[index]:
            copy.wait_recv()
        lax.fori_loop(*spans[index], add_arrived, 0)
        target, landing = ((before, STEPS + ROWS), (after, 0))[index]
        start = STEPS + spans[index][0]
        skip = index
        for level in range(2):
            at = level * skip
            copy = remote(
                fields.at[level, pl.ds(start + at, STEPS - level)],
                fields.at[level, pl.ds(landing + at, STEPS - level)],
                halo_send.at[index, level], halo_recv.at[index, level], {"strip": target},
            )
            copy.start()
            halos.append(copy)
    lax.fori_loop(*spans[2], for_other, 0)
    crossing.append(core_copies(2))
    for copy in crossing[2]:
        copy.start()
    lax.fori_loop(*spans[2], for_own, 0)
    for copy in crossing[2]:
        copy.wait_recv()
    lax.fori_loop(*spans[2], add_arrived, 0)
    for copy in halos:
        copy.wait_send()
    inner_sweeps(fields, speed, middle, False)
    for copy in halos:
        copy.wait_recv()

    for side, row0 in enumerate((0, STEPS + ROWS)):
        @pl.when(jnp.logical_not(inside[side]))
        def _():
            for level in range(2):
                for r in range(STEPS):
                    fields[level, row0 + r] = jnp.zeros((RANK, COLS), F32)

    edge_sweeps(fields, speed, middle, False)

    results = [
        pltpu.make_async_copy(fields.at[0, pl.ds(STEPS, ROWS)], s_out.at[own], out_sem.at[0]),
        remote(fields.at[0, pl.ds(STEPS, ROWS)], s_out.at[own], core_send.at[6], core_recv.at[6], {"shot": away}),
    ]
    for copy in results:
        copy.start()

    def gram_rows(i, total):
        value = jnp.concatenate([stacked(fields[0, STEPS + 4 * i + j]) for j in range(4)], 1)
        return total + dot_rows(value, value)

    gram = lax.fori_loop(0, ROWS // 4, gram_rows, jnp.zeros((2 * RANK, 2 * RANK), F32))
    gram = gram[:RANK] + gram[RANK:]
    gram = gram[:, :RANK] + gram[:, RANK:]
    gram = strip_sum(jnp.concatenate([gram, jnp.zeros((RANK, HALF - RANK), F32)], 1), 1)
    plane_send[2] = gram
    swap = remote(plane_send.at[2], other_gram, core_send.at[7], core_recv.at[7], {"shot": away})
    swap.start()
    swap.wait()
    theirs = other_gram[...]
    flag = (own + jnp.zeros((RANK, HALF), jnp.int32)) == 0
    inv_out[0] = lower_inverse(jnp.where(flag, gram, theirs))
    inv_out[1] = lower_inverse(jnp.where(flag, theirs, gram))

    for copy in results:
        copy.wait()
    for copy in edges:
        copy.wait_send()
    for copies in crossing:
        for copy in copies:
            copy.wait_send()


def final_kernel(scale, s_ref, inv_ref, left_out, right_out, blocks, sem):
    copies = []
    for side, out in enumerate((left_out, right_out)):
        inverse = inv_ref[side] * scale
        left = inverse[:, RANK : 2 * RANK]
        high, low = split(left)
        lhs = jnp.concatenate([jnp.concatenate([high, high], 1), jnp.concatenate([low, low], 1)], 0)

        def body(r, carry):
            both = dot(lhs, stacked(s_ref[side, r]))
            value = both[:RANK] + both[RANK:]
            for h in range(2):
                blocks[side, h, pl.ds(r, RANK, stride=ROWS), :] = value[:, h * HALF : (h + 1) * HALF]
            return carry

        lax.fori_loop(0, ROWS, body, 0, unroll=4)
        for h in range(2):
            copy = pltpu.make_async_copy(blocks.at[side, h], out.at[:, pl.ds(h * HALF, HALF)], sem.at[side, h])
            copy.start()
            copies.append(copy)
    for copy in copies:
        copy.wait()


def shards(source_now, source_prev, adjoint_now, adjoint_prev, courant, probe_left, probe_right):
    waves = [a.reshape(WAVES * ROWS, COLS) for a in (source_now, source_prev, adjoint_now, adjoint_prev)]
    any_spec = pl.BlockSpec(memory_space=pl.ANY)
    vmem_spec = pl.BlockSpec(memory_space=pltpu.VMEM)
    dma = pltpu.SemaphoreType.DMA
    sketch, inverse = pl.pallas_call(
        main_kernel,
        out_shape=(
            jax.ShapeDtypeStruct((2, ROWS, RANK, COLS), F32),
            jax.ShapeDtypeStruct((2, RANK, HALF), F32),
        ),
        in_specs=[any_spec] * 9,
        out_specs=(any_spec, vmem_spec),
        scratch_shapes=[
            pltpu.VMEM((4, 2, WAVES * ROWS, HALF), F32),
            pltpu.VMEM((4, ROWS, 2 * WAVES, COLS), BF16),
            pltpu.VMEM((2, 2, RANK * ROWS, HALF), F32),
            pltpu.VMEM((2, 2, 2, RANK, STEPS, HALF), F32),
            pltpu.VMEM((ROWS, COLS), F32),
            pltpu.VMEM((2, STEPS, COLS), F32),
            pltpu.VMEM((TALL, 8, COLS), F32),
            pltpu.VMEM((TALL, 8, COLS), F32),
            pltpu.VMEM((2, 2, TALL, RANK, COLS), F32),
            pltpu.VMEM((2, 2 * RANK, HALF), BF16),
            pltpu.VMEM((3, RANK, HALF), F32),
            pltpu.VMEM((2, PLANE - 1, RANK, HALF), F32),
            pltpu.VMEM((2, RANK, HALF), F32),
            pltpu.VMEM((2, SIDE - 1, RANK, HALF), F32),
            pltpu.VMEM((RANK, HALF), F32),
            pltpu.VMEM((2, TALL, RANK, COLS), F32),
            pltpu.VMEM((2, ROWS, RANK, COLS), F32),
            pltpu.VMEM((2, ROWS, RANK, COLS), F32),
            dma((13,)),
            dma((2, 5)),
            dma((2, 5)),
            dma((2, PLANE + SIDE - 2)),
            dma((2, PLANE + SIDE - 2)),
            dma((8,)),
            dma((8,)),
            dma((2, 2)),
            dma((2, 2)),
            dma((1,)),
        ],
        compiler_params=pltpu.CompilerParams(
            collective_id=0, has_side_effects=True, vmem_limit_bytes=56 * 1024 * 1024
        ),
        name="sketch",
    )(*waves, courant, probe_left, probe_right, probe_left.reshape(RANK * ROWS, COLS), probe_right.reshape(RANK * ROWS, COLS))
    scale = math.sqrt(ROWS * lax.axis_size("strip") * COLS)
    outs = pl.pallas_call(
        functools.partial(final_kernel, scale),
        out_shape=(jax.ShapeDtypeStruct((RANK * ROWS, COLS), F32),) * 2,
        in_specs=[vmem_spec] * 2,
        out_specs=(any_spec, any_spec),
        scratch_shapes=[pltpu.VMEM((2, 2, RANK * ROWS, HALF), F32), dma((2, 2))],
        name="factors",
    )(sketch, inverse)
    return tuple(out.reshape(RANK, ROWS, COLS) for out in outs)


def solution(mesh):
    return jax.shard_map(
        shards,
        mesh=mesh,
        in_specs=(P("shot", None, "strip", None),) * 4 + (P("strip", None),) + (P(None, "strip", None),) * 2,
        out_specs=(P(None, "strip", None), P(None, "strip", None)),
        check_vma=False,
    )
```

time: 902 us -> 108 us (0.12)
  the two profiles are of different devices: /device:TPU:0 before, /device:TPU:1 now
where the time goes in v1:
time: 108 us
  Pallas kernels  107 us (99%)
    pallas_call x1, Pallas kernels, shards(): pl.pallas_call(main_kernel, out_shape=(jax.ShapeDtypeStruct((2, ROWS, RAN...  102 us
    pallas_call x1, Pallas kernels, shards(): pl.pallas_call(functools.partial(final_kernel, scale), out_shape=(jax.Sha...  4.86 us

profile of v1, /device:TPU:1, one launch (start us, length us, event | category | flops | bytes accessed | tf_op | source)
XLA Modules:
  0.0 107.7 jit_solution(5542239523290112414)
XLA Ops:
  0.6 102.2 %sketch.1 = (f32[2,32,16,256]{3,2,1,0:T(8,128)}, f32[2,16,128]{2,1,0:T(8,128)}) custom-call(f32[2048,256]{1,0:T(8,128)} %bitcast.8, f32[2048,256]{1,0:T(8,128)} %bitcast.9, f32[2048,256]{1,0:T(8,128)} %bitcast.10, f32[2048,256]{1,0:T(8,128)} %bitcast.11, f32[32,256]{1,0:T(8,128)} %courant.1, f32[16,32,256]{2,1,0:T(8,128)} %left3.1, f32[16,32,256]{2,1,0:T(8,128)} %right3.1, ...), custom_call_target="tpu_custom_call" | custom-call | tf_op jit(solution)/shard_map/sketch/pallas_call | solution.py:425
  102.8 4.9 %factors.1 = (f32[512,256]{1,0:T(8,128)}, f32[512,256]{1,0:T(8,128)}) custom-call(f32[2,32,16,256]{3,2,1,0:T(8,128)} %get-tuple-element.6.s_ref, f32[2,16,128]{2,1,0:T(8,128)} %get-tuple-element.7.inv_ref), custom_call_target="tpu_custom_call" | custom-call | tf_op jit(solution)/shard_map/factors/pallas_call | solution.py:469

commit v2 on v1

v2 whole, which is shorter than its diff:
```python
import functools
import math

import jax
import jax.numpy as jnp
from jax import lax
from jax.experimental import pallas as pl
from jax.experimental.pallas import tpu as pltpu
from jax.sharding import PartitionSpec as P

STEPS = 8
WAVES = 64
RANK = 16
ROWS = 32
COLS = 256
HALF = 128
TALL = ROWS + 2 * STEPS
SIDE = 4
PLANE = SIDE * SIDE
MESH = pl.DeviceIdType.MESH
F32 = jnp.float32
BF16 = jnp.bfloat16


def split(x):
    high = x.astype(BF16)
    low = (x - high.astype(F32)).astype(BF16)
    return high, low


def stacked(x):
    return jnp.concatenate(split(x), 0)


def dot_rows(a, b):
    return lax.dot_general(a, b, (((1,), (1,)), ((), ())), preferred_element_type=F32)


def dot(a, b):
    return lax.dot_general(a, b, (((1,), (0,)), ((), ())), preferred_element_type=F32)


def spread_of(cells, beside):
    count = cells.shape[0]
    both = dot(jnp.concatenate(split(cells.reshape(count * RANK, COLS)), 0), beside[...])
    return (both[: count * RANK] + both[count * RANK :]).reshape(count, 2, 8, COLS)


def load_rows(ref, low, count):
    return ref[pl.ds(low, count)].reshape(count, 2, 8, COLS)


def advance(buf, speed, middle, beside, level, starts, count, transposed):
    now = buf.at[lax.rem(level + 1, 2)]
    new = buf.at[lax.rem(level, 2)]
    pieces = []
    for low in starts:
        cells = load_rows(now, low - 1, count + 2)
        if transposed:
            cells = cells * speed[pl.ds(low - 1, count + 2)][:, None]
        pieces.append(cells)
    inner = [cells[1:-1] for cells in pieces]
    side = spread_of(inner[0] if len(inner) == 1 else jnp.concatenate(inner, 0), beside)
    for k, low in enumerate(starts):
        total = pieces[k][:-2] + pieces[k][2:] + side[k * count : (k + 1) * count]
        if not transposed:
            total = total * speed[pl.ds(low, count)][:, None]
        centre = load_rows(now, low, count) if transposed else inner[k]
        value = middle[pl.ds(low, count)][:, None] * centre - load_rows(new, low, count) + total
        new[pl.ds(low, count)] = value.reshape(count, RANK, COLS)


def inner_sweeps(buf, speed, middle, beside, transposed):
    for level in range(1, STEPS + 1):
        advance(buf, speed, middle, beside, level, (STEPS + level,), ROWS - 2 * level, transposed)


def edge_sweeps(buf, speed, middle, beside, transposed):
    def body(level, carry):
        advance(buf, speed, middle, beside, level, (level, STEPS + ROWS - level), STEPS, transposed)
        return carry

    lax.fori_loop(1, STEPS + 1, body, 0)


def lower_inverse(gram):
    row = lax.broadcasted_iota(jnp.int32, (RANK, HALF), 0)
    lane = lax.broadcasted_iota(jnp.int32, (RANK, HALF), 1)
    work = jnp.where(lane < RANK, gram, jnp.where(lane == row + RANK, 1.0, 0.0))
    for k in range(RANK):
        pivot = work[k : k + 1, k : k + 1]
        root = 1.0 / jnp.sqrt(pivot)
        line = work[k : k + 1, :] * root
        column = jnp.where(row[:, :1] > k, work[:, k : k + 1] * root, 0.0)
        work = jnp.where(row == k, line, work - column * line)
    return work


def main_kernel(
    src_now, src_prev, adj_now, adj_prev, courant, probe_left, probe_right,
    s_out, inv_out,
    waves, slabs, probes, probe_edges, speed_own, speed_edges, speed, middle, beside,
    steps_p, steps_other, weights, plane_send, plane_recv, column_send, column_recv, other_gram,
    fields, leaving, partial, arrived,
    load_sem, edge_send, edge_recv, sum_send, sum_recv, core_send, core_recv, halo_send, halo_recv,
    step_send, step_recv, out_sem,
):
    own = lax.axis_index("shot")
    away = 1 - own
    me = lax.axis_index("strip")
    count = lax.axis_size("strip")
    x, y, z = me % SIDE, (me // SIDE) % SIDE, me // PLANE
    after, before = (me + 1) % count, (me + count - 1) % count
    lane = lax.broadcasted_iota(jnp.int32, (RANK, HALF), 1)
    blocks = ROWS // STEPS
    targets = ((after, ROWS - STEPS), (before, 0))
    halves = [pl.ds(0, HALF), pl.ds(HALF, HALF)]

    def plane_peer(d):
        return z * PLANE + ((y + d // SIDE) % SIDE) * SIDE + (x + d % SIDE) % SIDE

    def column_peer(d):
        return ((z + d) % SIDE) * PLANE + y * SIDE + x

    def remote(src, dst, send, recv, device):
        return pltpu.make_async_remote_copy(
            src_ref=src, dst_ref=dst, send_sem=send, recv_sem=recv, device_id=device, device_id_type=MESH
        )

    barrier = pltpu.get_barrier_semaphore()
    strips = [plane_peer(d) for d in range(1, PLANE)] + [column_peer(d) for d in range(1, SIDE)] + [after, before]
    for peer in strips:
        pl.semaphore_signal(barrier, inc=1, device_id={"strip": peer}, device_id_type=MESH)
    pl.semaphore_signal(barrier, inc=1, device_id={"shot": away}, device_id_type=MESH)

    def probe_loads(probe):
        return [
            pltpu.make_async_copy(probe.at[:, pl.ds(b * STEPS, STEPS), halves[h]], probes.at[b, h], load_sem.at[1 + 2 * b + h])
            for b in range(blocks)
            for h in range(2)
        ]

    def probe_sends(probe):
        return [
            remote(probe.at[:, pl.ds(first, STEPS), halves[h]], probe_edges.at[side, h],
                   edge_send.at[side, 1 + h], edge_recv.at[side, 1 + h], {"strip": target})
            for side, (target, first) in enumerate(targets)
            for h in range(2)
        ]

    load_speed = pltpu.make_async_copy(courant, speed_own, load_sem.at[0])
    load_speed.start()
    for core, probe in enumerate((probe_left, probe_right)):
        @pl.when(own == core)
        def _():
            for load in probe_loads(probe):
                load.start()
    base = 1 + 2 * blocks
    loads = [
        [
            pltpu.make_async_copy(
                wave.at[:, pl.ds(b * STEPS, STEPS), halves[h]], waves.at[a, b, h],
                load_sem.at[base + (a * blocks + b) * 2 + h],
            )
            for b in range(blocks)
            for h in range(2)
        ]
        for a, wave in enumerate((src_now, src_prev, adj_now, adj_prev))
    ]
    for group in loads:
        for load in group:
            load.start()

    near = lax.broadcasted_iota(jnp.int32, (COLS, COLS), 0) - lax.broadcasted_iota(jnp.int32, (COLS, COLS), 1)
    beside[...] = jnp.where(jnp.abs(near) == 1, 1.0, 0.0).astype(BF16)

    def put_speed(values, row0):
        for r in range(STEPS):
            value = jnp.broadcast_to(values[r : r + 1, :], (8, COLS))
            speed[row0 + r] = value
            middle[row0 + r] = 2.0 - 4.0 * value

    load_speed.wait()
    for block in range(blocks):
        put_speed(speed_own[pl.ds(block * STEPS, STEPS), :], STEPS + block * STEPS)
    for load in probe_loads(probe_left):
        load.wait()

    def rows_of(tiles, b, r):
        return jnp.concatenate([
            tiles.at[b, h].reshape(RANK * STEPS, HALF)[pl.ds(r, RANK, stride=STEPS), :] for h in range(2)
        ], 1)

    for b in range(blocks):
        for r in range(STEPS):
            steps_p[0, STEPS + b * STEPS + r] = rows_of(probes, b, r)

    def put_zero(r, carry):
        steps_p[1, r] = jnp.zeros((RANK, COLS), F32)
        return carry

    lax.fori_loop(0, TALL, put_zero, 0)

    pl.semaphore_wait(barrier, len(strips) + 1)

    speed_sends = [
        remote(courant.at[pl.ds(first, STEPS)], speed_edges.at[side],
               edge_send.at[side, 0], edge_recv.at[side, 0], {"strip": target})
        for side, (target, first) in enumerate(targets)
    ]
    for copy in speed_sends:
        copy.start()
    for core, probe in enumerate((probe_left, probe_right)):
        @pl.when(own == core)
        def _():
            for copy in probe_sends(probe):
                copy.start()
    edges = speed_sends + probe_sends(probe_left)

    inner_sweeps(steps_p, speed, middle, beside, True)

    spans = ((0, STEPS), (ROWS - STEPS, ROWS), (STEPS, ROWS - STEPS))

    def hand_over(index):
        lo, hi = spans[index]
        copies = [
            remote(steps_p.at[level, pl.ds(STEPS + lo, hi - lo)], steps_other.at[level, pl.ds(lo, hi - lo)],
                   step_send.at[index, level], step_recv.at[index, level], {"shot": away})
            for level in range(2)
        ]
        for copy in copies:
            copy.start()
        return copies

    handed = {2: hand_over(2)}

    for a in range(4):
        for load in loads[a]:
            load.wait()
        for b in range(blocks):
            def put_slab(r, carry):
                value = jnp.concatenate([
                    waves.at[a, b, h].reshape(WAVES * STEPS, HALF)[pl.ds(r, WAVES, stride=STEPS), :] for h in range(2)
                ], 1)
                slabs[a, b * STEPS + r] = stacked(value)
                return carry

            lax.fori_loop(0, STEPS, put_slab, 0)

    def own_products(r, total):
        a = 2 - 2 * own
        total = total + dot_rows(stacked(steps_p[0, STEPS + r]), slabs[a, r])
        return total - dot_rows(stacked(steps_p[1, STEPS + r]), slabs[a + 1, r])

    def other_products(r, total):
        a = 2 * own
        total = total + dot_rows(stacked(steps_other[0, r]), slabs[a, r])
        return total - dot_rows(stacked(steps_other[1, r]), slabs[a + 1, r])

    zero = jnp.zeros((2 * RANK, HALF), F32)
    mine = lax.fori_loop(*spans[2], own_products, zero, unroll=2)
    for copy in handed[2]:
        copy.wait_recv()
    theirs = lax.fori_loop(*spans[2], other_products, zero, unroll=2)

    for copy in edges:
        copy.wait_recv()
    inside = (me > 0, me < count - 1)
    for side, row0 in enumerate((0, STEPS + ROWS)):
        put_speed(jnp.where(inside[side], speed_edges[side], 0.0), row0)
        for r in range(STEPS):
            steps_p[0, row0 + r] = rows_of(probe_edges, side, r)
    edge_sweeps(steps_p, speed, middle, beside, True)
    for index in range(2):
        handed[index] = hand_over(index)
    for index in range(2):
        mine = lax.fori_loop(*spans[index], own_products, mine, unroll=2)
    for index in range(2):
        for copy in handed[index]:
            copy.wait_recv()
        theirs = lax.fori_loop(*spans[index], other_products, theirs, unroll=2)

    def strip_sum(value, i):
        plane_send[i] = value
        copies = [
            remote(plane_send.at[i], plane_recv.at[i, d - 1], sum_send.at[i, d - 1], sum_recv.at[i, d - 1],
                   {"strip": plane_peer(d)})
            for d in range(1, PLANE)
        ]
        for copy in copies:
            copy.start()
        for d, copy in enumerate(copies):
            copy.wait_recv()
            value = value + plane_recv[i, d]
        column_send[i] = value
        more = [
            remote(column_send.at[i], column_recv.at[i, d - 1], sum_send.at[i, PLANE + d - 2],
                   sum_recv.at[i, PLANE + d - 2], {"strip": column_peer(d)})
            for d in range(1, SIDE)
        ]
        for copy in more:
            copy.start()
        for d, copy in enumerate(more):
            copy.wait_recv()
            value = value + column_recv[i, d]
        for copy in copies + more:
            copy.wait_send()
        return value

    folded = []
    for total in (mine, theirs):
        both = total[:RANK] + total[RANK:]
        folded.append(both + pltpu.roll(both, WAVES, 1))
    weight = strip_sum(jnp.where(lane < WAVES, folded[0], folded[1]), 0)
    turned = pltpu.roll(weight, WAVES, 1)
    weights[0] = stacked(jnp.where(lane < WAVES, weight, turned))
    weights[1] = stacked(jnp.where(lane < WAVES, turned, weight))

    def combine(which, level, r):
        side = away if which else own
        both = dot(weights[which], slabs[2 * side + level, r])
        return both[:RANK] + both[RANK:]

    def for_other(r, carry):
        for level in range(2):
            partial[level, r] = combine(1, level, r)
        return carry

    def for_own(r, carry):
        for level in range(2):
            fields[level, STEPS + r] = combine(0, level, r)
        return carry

    def add_arrived(r, carry):
        for level in range(2):
            fields[level, STEPS + r] = fields[level, STEPS + r] + arrived[level, r]
        return carry

    def core_copies(index):
        lo, hi = spans[index]
        copies = [
            remote(partial.at[level, pl.ds(lo, hi - lo)], arrived.at[level, pl.ds(lo, hi - lo)],
                   core_send.at[2 * index + level], core_recv.at[2 * index + level], {"shot": away})
            for level in range(2)
        ]
        for copy in copies:
            copy.start()
        return copies

    crossing = []
    for index in range(2):
        lax.fori_loop(*spans[index], for_other, 0, unroll=2)
        crossing.append(core_copies(index))
    halos = []
    for index in range(2):
        lax.fori_loop(*spans[index], for_own, 0, unroll=2)
    for index in range(2):
        for copy in crossing[index]:
            copy.wait_recv()
        lo = spans[index][0]

        def add_edge(r, carry):
            for level in range(2):
                value = fields[level, STEPS + lo + r] + arrived[level, lo + r]
                fields[level, STEPS + lo + r] = value
                leaving[index, level, r] = value
            return carry

        lax.fori_loop(0, STEPS, add_edge, 0)
        target, landing = ((before, STEPS + ROWS), (after, 0))[index]
        for level in range(2):
            at = level * index
            copy = remote(
                leaving.at[index, level, pl.ds(at, STEPS - level)],
                fields.at[level, pl.ds(landing + at, STEPS - level)],
                halo_send.at[index, level], halo_recv.at[index, level], {"strip": target},
            )
            copy.start()
            halos.append(copy)
    lax.fori_loop(*spans[2], for_other, 0, unroll=2)
    crossing.append(core_copies(2))
    lax.fori_loop(*spans[2], for_own, 0, unroll=2)
    for copy in crossing[2]:
        copy.wait_recv()
    lax.fori_loop(*spans[2], add_arrived, 0)
    inner_sweeps(fields, speed, middle, beside, False)
    for copy in halos:
        copy.wait_recv()

    for side, row0 in enumerate((0, STEPS + ROWS)):
        @pl.when(jnp.logical_not(inside[side]))
        def _():
            for level in range(2):
                for r in range(STEPS):
                    fields[level, row0 + r] = jnp.zeros((RANK, COLS), F32)

    edge_sweeps(fields, speed, middle, beside, False)

    results = [
        pltpu.make_async_copy(fields.at[0, pl.ds(STEPS, ROWS)], s_out.at[own], out_sem.at[0]),
        remote(fields.at[0, pl.ds(STEPS, ROWS)], s_out.at[own], core_send.at[6], core_recv.at[6], {"shot": away}),
    ]
    for copy in results:
        copy.start()

    def gram_rows(i, total):
        value = jnp.concatenate([stacked(fields[0, STEPS + 4 * i + j]) for j in range(4)], 1)
        return total + dot_rows(value, value)

    gram = lax.fori_loop(0, ROWS // 4, gram_rows, jnp.zeros((2 * RANK, 2 * RANK), F32))
    gram = gram[:RANK] + gram[RANK:]
    gram = gram[:, :RANK] + gram[:, RANK:]
    gram = strip_sum(jnp.concatenate([gram, jnp.zeros((RANK, HALF - RANK), F32)], 1), 1)
    plane_send[2] = gram
    swap = remote(plane_send.at[2], other_gram, core_send.at[7], core_recv.at[7], {"shot": away})
    swap.start()
    swap.wait()
    theirs = other_gram[...]
    flag = (own + jnp.zeros((RANK, HALF), jnp.int32)) == 0
    inv_out[0] = lower_inverse(jnp.where(flag, gram, theirs))
    inv_out[1] = lower_inverse(jnp.where(flag, theirs, gram))

    for copy in results:
        copy.wait()
    for copy in edges + halos:
        copy.wait_send()
    for copies in crossing + list(handed.values()):
        for copy in copies:
            copy.wait_send()


def final_kernel(scale, s_hbm, inv_ref, left_out, right_out, sketch, blocks, load_sem, sem):
    count = ROWS // STEPS
    loads = {}
    for b in range(count):
        for side in range(2):
            loads[b, side] = pltpu.make_async_copy(
                s_hbm.at[side, pl.ds(b * STEPS, STEPS)], sketch.at[side, b], load_sem.at[side, b]
            )
            loads[b, side].start()
    lhs = []
    for side in range(2):
        high, low = split((inv_ref[side] * scale)[:, RANK : 2 * RANK])
        lhs.append(jnp.concatenate([jnp.concatenate([high, high], 1), jnp.concatenate([low, low], 1)], 0))
    copies = []
    for b in range(count):
        for side, out in enumerate((left_out, right_out)):
            loads[b, side].wait()
            for r in range(STEPS):
                both = dot(lhs[side], stacked(sketch[side, b, r]))
                value = both[:RANK] + both[RANK:]
                for h in range(2):
                    blocks.at[side, b, h].reshape(RANK * STEPS, HALF)[pl.ds(r, RANK, stride=STEPS), :] = (
                        value[:, h * HALF : (h + 1) * HALF]
                    )
            for h in range(2):
                copy = pltpu.make_async_copy(
                    blocks.at[side, b, h],
                    out.at[:, pl.ds(b * STEPS, STEPS), pl.ds(h * HALF, HALF)],
                    sem.at[side, b, h],
                )
                copy.start()
                copies.append(copy)
    for copy in copies:
        copy.wait()


def shards(source_now, source_prev, adjoint_now, adjoint_prev, courant, probe_left, probe_right):
    waves = [a.reshape(WAVES, ROWS, COLS) for a in (source_now, source_prev, adjoint_now, adjoint_prev)]
    any_spec = pl.BlockSpec(memory_space=pl.ANY)
    vmem_spec = pl.BlockSpec(memory_space=pltpu.VMEM)
    dma = pltpu.SemaphoreType.DMA
    count = ROWS // STEPS
    sketch, inverse = pl.pallas_call(
        main_kernel,
        out_shape=(
            jax.ShapeDtypeStruct((2, ROWS, RANK, COLS), F32),
            jax.ShapeDtypeStruct((2, RANK, HALF), F32),
        ),
        in_specs=[any_spec] * 7,
        out_specs=(any_spec, vmem_spec),
        scratch_shapes=[
            pltpu.VMEM((4, count, 2, WAVES, STEPS, HALF), F32),
            pltpu.VMEM((4, ROWS, 2 * WAVES, COLS), BF16),
            pltpu.VMEM((count, 2, RANK, STEPS, HALF), F32),
            pltpu.VMEM((2, 2, RANK, STEPS, HALF), F32),
            pltpu.VMEM((ROWS, COLS), F32),
            pltpu.VMEM((2, STEPS, COLS), F32),
            pltpu.VMEM((TALL, 8, COLS), F32),
            pltpu.VMEM((TALL, 8, COLS), F32),
            pltpu.VMEM((COLS, COLS), BF16),
            pltpu.VMEM((2, TALL, RANK, COLS), F32),
            pltpu.VMEM((2, ROWS, RANK, COLS), F32),
            pltpu.VMEM((2, 2 * RANK, HALF), BF16),
            pltpu.VMEM((3, RANK, HALF), F32),
            pltpu.VMEM((2, PLANE - 1, RANK, HALF), F32),
            pltpu.VMEM((2, RANK, HALF), F32),
            pltpu.VMEM((2, SIDE - 1, RANK, HALF), F32),
            pltpu.VMEM((RANK, HALF), F32),
            pltpu.VMEM((2, TALL, RANK, COLS), F32),
            pltpu.VMEM((2, 2, STEPS, RANK, COLS), F32),
            pltpu.VMEM((2, ROWS, RANK, COLS), F32),
            pltpu.VMEM((2, ROWS, RANK, COLS), F32),
            dma((1 + 2 * count + 8 * count,)),
            dma((2, 3)),
            dma((2, 3)),
            dma((2, PLANE + SIDE - 2)),
            dma((2, PLANE + SIDE - 2)),
            dma((8,)),
            dma((8,)),
            dma((2, 2)),
            dma((2, 2)),
            dma((3, 2)),
            dma((3, 2)),
            dma((1,)),
        ],
        compiler_params=pltpu.CompilerParams(
            collective_id=0, has_side_effects=True, vmem_limit_bytes=56 * 1024 * 1024
        ),
        name="sketch",
    )(*waves, courant, probe_left, probe_right)
    scale = math.sqrt(ROWS * lax.axis_size("strip") * COLS)
    return pl.pallas_call(
        functools.partial(final_kernel, scale),
        out_shape=(jax.ShapeDtypeStruct((RANK, ROWS, COLS), F32),) * 2,
        in_specs=[any_spec, vmem_spec],
        out_specs=(any_spec, any_spec),
        scratch_shapes=[
            pltpu.VMEM((2, count, STEPS, RANK, COLS), F32),
            pltpu.VMEM((2, count, 2, RANK, STEPS, HALF), F32),
            dma((2, count)),
            dma((2, count, 2)),
        ],
        name="factors",
    )(sketch, inverse)


def solution(mesh):
    return jax.shard_map(
        shards,
        mesh=mesh,
        in_specs=(P("shot", None, "strip", None),) * 4 + (P("strip", None),) + (P(None, "strip", None),) * 2,
        out_specs=(P(None, "strip", None), P(None, "strip", None)),
        check_vma=False,
    )
```

time: 108 us -> 62.8 us (0.58)
  Pallas kernels: 107 us -> 62 us
    pallas_call x1, Pallas kernels: 102 us -> 58.1 us  [shards(): pl.pallas_call(main_kernel, out_shape=(jax.ShapeDtypeStruct((2, ROWS, RAN...]
where the time goes in v2:
time: 62.8 us; the launch traced here: 62.7 us
  Pallas kernels  62 us (99%)
  between operations  0.64 us (1%)
    pallas_call x1, Pallas kernels, shards(): pl.pallas_call(main_kernel, out_shape=(jax.ShapeDtypeStruct((2, ROWS, RAN...  58.1 us
    pallas_call x1, Pallas kernels, shards(): pl.pallas_call(functools.partial(final_kernel, scale), out_shape=(jax.Sha...  3.88 us

profile of v2, /device:TPU:1, one launch (start us, length us, event | category | flops | bytes accessed | tf_op | source)
XLA Modules:
  0.0 62.7 jit_solution(4653358395187286007)
XLA Ops:
  0.6 58.1 %sketch.1 = (f32[2,32,16,256]{3,2,1,0:T(8,128)}, f32[2,16,128]{2,1,0:T(8,128)}) custom-call(f32[64,32,256]{2,1,0:T(8,128)} %bitcast.4, f32[64,32,256]{2,1,0:T(8,128)} %bitcast.5, f32[64,32,256]{2,1,0:T(8,128)} %bitcast.6, f32[64,32,256]{2,1,0:T(8,128)} %bitcast.7, f32[32,256]{1,0:T(8,128)} %courant.1, f32[16,32,256]{2,1,0:T(8,128)} %probe_left.1, ...), custom_call_target="tpu_custom_call" | custom-call | tf_op jit(solution)/shard_map/sketch/pallas_call | solution.py:474
  58.8 3.9 %factors.1 = (f32[16,32,256]{2,1,0:T(8,128)}, f32[16,32,256]{2,1,0:T(8,128)}) custom-call(f32[2,32,16,256]{3,2,1,0:T(8,128)} %get-tuple-element.4.s_hbm, f32[2,16,128]{2,1,0:T(8,128)} %get-tuple-element.5.inv_ref), custom_call_target="tpu_custom_call" | custom-call | tf_op jit(solution)/shard_map/factors/pallas_call | solution.py:523

commit v3 on v2

--- a/solution.py
+++ b/solution.py
@@ -18,6 +18,14 @@
 SIDE = 4
 PLANE = SIDE * SIDE
 MESH = pl.DeviceIdType.MESH
+
+
+def hops(d):
+    return sum(min(k, SIDE - k) for k in (d % SIDE, d // SIDE))
+
+
+FAR_FIRST = sorted(range(1, PLANE), key=lambda d: -hops(d))
+COLUMN_FIRST = (2, 1, 3)
 F32 = jnp.float32
 BF16 = jnp.bfloat16
 
@@ -97,13 +105,13 @@
 
 
 def main_kernel(
-    src_now, src_prev, adj_now, adj_prev, courant, probe_left, probe_right,
-    s_out, inv_out,
+    scale, src_now, src_prev, adj_now, adj_prev, courant, probe_left, probe_right,
+    left_out, right_out,
     waves, slabs, probes, probe_edges, speed_own, speed_edges, speed, middle, beside,
-    steps_p, steps_other, weights, plane_send, plane_recv, column_send, column_recv, other_gram,
+    steps_p, steps_other, weights, plane_send, plane_recv, column_send, column_recv, gram_send, gram_recv, pair_send, pair_recv, sketches, inverses,
     fields, leaving, partial, arrived,
     load_sem, edge_send, edge_recv, sum_send, sum_recv, core_send, core_recv, halo_send, halo_recv,
-    step_send, step_recv, out_sem,
+    step_send, step_recv, keep_sem,
 ):
     own = lax.axis_index("shot")
     away = 1 - own
@@ -128,10 +136,12 @@
         )
 
     barrier = pltpu.get_barrier_semaphore()
-    strips = [plane_peer(d) for d in range(1, PLANE)] + [column_peer(d) for d in range(1, SIDE)] + [after, before]
+    strips = [after, before] + [plane_peer(d) for d in FAR_FIRST] + [column_peer(d) for d in COLUMN_FIRST]
     for peer in strips:
         pl.semaphore_signal(barrier, inc=1, device_id={"strip": peer}, device_id_type=MESH)
     pl.semaphore_signal(barrier, inc=1, device_id={"shot": away}, device_id_type=MESH)
+    for d in FAR_FIRST:
+        pl.semaphore_signal(barrier, inc=1, device_id={"strip": plane_peer(d), "shot": away}, device_id_type=MESH)
 
     def probe_loads(probe):
         return [
@@ -201,7 +211,7 @@
 
     lax.fori_loop(0, TALL, put_zero, 0)
 
-    pl.semaphore_wait(barrier, len(strips) + 1)
+    pl.semaphore_wait(barrier, len(strips) + PLANE)
 
     speed_sends = [
         remote(courant.at[pl.ds(first, STEPS)], speed_edges.at[side],
@@ -258,10 +268,7 @@
         return total - dot_rows(stacked(steps_other[1, r]), slabs[a + 1, r])
 
     zero = jnp.zeros((2 * RANK, HALF), F32)
-    mine = lax.fori_loop(*spans[2], own_products, zero, unroll=2)
-    for copy in handed[2]:
-        copy.wait_recv()
-    theirs = lax.fori_loop(*spans[2], other_products, zero, unroll=2)
+    mine = lax.fori_loop(*spans[2], own_products, zero, unroll=4)
 
     for copy in edges:
         copy.wait_recv()
@@ -273,45 +280,72 @@
     edge_sweeps(steps_p, speed, middle, beside, True)
     for index in range(2):
         handed[index] = hand_over(index)
+    for copy in handed[2]:
+        copy.wait_recv()
+    theirs = lax.fori_loop(*spans[2], other_products, zero, unroll=4)
     for index in range(2):
-        mine = lax.fori_loop(*spans[index], own_products, mine, unroll=2)
+        mine = lax.fori_loop(*spans[index], own_products, mine, unroll=4)
     for index in range(2):
         for copy in handed[index]:
             copy.wait_recv()
-        theirs = lax.fori_loop(*spans[index], other_products, theirs, unroll=2)
-
-    def strip_sum(value, i):
-        plane_send[i] = value
-        copies = [
-            remote(plane_send.at[i], plane_recv.at[i, d - 1], sum_send.at[i, d - 1], sum_recv.at[i, d - 1],
-                   {"strip": plane_peer(d)})
-            for d in range(1, PLANE)
-        ]
-        for copy in copies:
-            copy.start()
-        for d, copy in enumerate(copies):
-            copy.wait_recv()
-            value = value + plane_recv[i, d]
-        column_send[i] = value
-        more = [
-            remote(column_send.at[i], column_recv.at[i, d - 1], sum_send.at[i, PLANE + d - 2],
-                   sum_recv.at[i, PLANE + d - 2], {"strip": column_peer(d)})
-            for d in range(1, SIDE)
-        ]
-        for copy in more:
-            copy.start()
-        for d, copy in enumerate(more):
-            copy.wait_recv()
-            value = value + column_recv[i, d]
-        for copy in copies + more:
+        theirs = lax.fori_loop(*spans[index], other_products, theirs, unroll=4)
+
+    def start(src, dst, k, device):
+        copy = remote(src, dst, sum_send.at[k], sum_recv.at[k], device)
+        copy.start()
+        return copy
+
+    def strip_sum(value):
+        plane_send[...] = value
+        copies = {d: start(plane_send, plane_recv.at[d - 1], d - 1, {"strip": plane_peer(d)}) for d in FAR_FIRST}
+        for d in range(1, PLANE):
+            copies[d].wait_recv()
+            value = value + plane_recv[d - 1]
+        column_send[...] = value
+        more = {
+            d: start(column_send, column_recv.at[d - 1], PLANE + d - 2, {"strip": column_peer(d)}) for d in COLUMN_FIRST
+        }
+        for d in range(1, SIDE):
+            more[d].wait_recv()
+            value = value + column_recv[d - 1]
+        for copy in list(copies.values()) + list(more.values()):
             copy.wait_send()
         return value
+
+    def gram_sum(value):
+        first = PLANE + SIDE - 2
+        gram_send[...] = value
+        copies = {}
+        for d in FAR_FIRST:
+            copies[0, d] = start(gram_send, gram_recv.at[0, d], first + d, {"strip": plane_peer(d)})
+            copies[1, d] = start(gram_send, gram_recv.at[1, d], first + PLANE + d, {"strip": plane_peer(d), "shot": away})
+        copies[1, 0] = start(gram_send, gram_recv.at[1, 0], first + PLANE, {"shot": away})
+        for d in range(1, PLANE):
+            copies[0, d].wait_recv()
+            value = value + gram_recv[0, d]
+        copies[1, 0].wait_recv()
+        other = gram_recv[1, 0]
+        for d in range(1, PLANE):
+            copies[1, d].wait_recv()
+            other = other + gram_recv[1, d]
+        pair = [value, other]
+        for k in range(2):
+            pair_send[k] = pair[k]
+        more = {}
+        for d in COLUMN_FIRST:
+            more[d] = start(pair_send, pair_recv.at[d - 1], first + 2 * PLANE + d - 1, {"strip": column_peer(d)})
+        for d in range(1, SIDE):
+            more[d].wait_recv()
+            pair = [pair[k] + pair_recv[d - 1, k] for k in range(2)]
+        for copy in list(copies.values()) + list(more.values()):
+            copy.wait_send()
+        return pair
 
     folded = []
     for total in (mine, theirs):
         both = total[:RANK] + total[RANK:]
         folded.append(both + pltpu.roll(both, WAVES, 1))
-    weight = strip_sum(jnp.where(lane < WAVES, folded[0], folded[1]), 0)
+    weight = strip_sum(jnp.where(lane < WAVES, folded[0], folded[1]))
     turned = pltpu.roll(weight, WAVES, 1)
     weights[0] = stacked(jnp.where(lane < WAVES, weight, turned))
     weights[1] = stacked(jnp.where(lane < WAVES, turned, weight))
@@ -321,54 +355,38 @@
         both = dot(weights[which], slabs[2 * side + level, r])
         return both[:RANK] + both[RANK:]
 
-    def for_other(r, carry):
-        for level in range(2):
-            partial[level, r] = combine(1, level, r)
+    def for_other(level, r, carry):
+        partial[level, r] = combine(1, level, r)
         return carry
 
-    def for_own(r, carry):
-        for level in range(2):
-            fields[level, STEPS + r] = combine(0, level, r)
+    def for_own(level, r, carry):
+        fields[level, STEPS + r] = combine(0, level, r)
         return carry
 
-    def add_arrived(r, carry):
-        for level in range(2):
-            fields[level, STEPS + r] = fields[level, STEPS + r] + arrived[level, r]
-        return carry
-
-    def core_copies(index):
+    def cross(level, index):
         lo, hi = spans[index]
-        copies = [
-            remote(partial.at[level, pl.ds(lo, hi - lo)], arrived.at[level, pl.ds(lo, hi - lo)],
-                   core_send.at[2 * index + level], core_recv.at[2 * index + level], {"shot": away})
-            for level in range(2)
-        ]
-        for copy in copies:
-            copy.start()
-        return copies
-
-    crossing = []
-    for index in range(2):
-        lax.fori_loop(*spans[index], for_other, 0, unroll=2)
-        crossing.append(core_copies(index))
+        copy = remote(
+            partial.at[level, pl.ds(lo, hi - lo)], arrived.at[level, pl.ds(lo, hi - lo)],
+            core_send.at[2 * index + level], core_recv.at[2 * index + level], {"shot": away},
+        )
+        copy.start()
+        return copy
+
+    crossing = {}
+    for level in range(2):
+        for index in range(2):
+            lax.fori_loop(*spans[index], functools.partial(for_other, level), 0, unroll=8)
+            crossing[level, index] = cross(level, index)
     halos = []
-    for index in range(2):
-        lax.fori_loop(*spans[index], for_own, 0, unroll=2)
-    for index in range(2):
-        for copy in crossing[index]:
-            copy.wait_recv()
-        lo = spans[index][0]
-
-        def add_edge(r, carry):
-            for level in range(2):
-                value = fields[level, STEPS + lo + r] + arrived[level, lo + r]
-                fields[level, STEPS + lo + r] = value
-                leaving[index, level, r] = value
-            return carry
-
-        lax.fori_loop(0, STEPS, add_edge, 0)
-        target, landing = ((before, STEPS + ROWS), (after, 0))[index]
-        for level in range(2):
+    for level in range(2):
+        for index in range(2):
+            lax.fori_loop(*spans[index], functools.partial(for_own, level), 0, unroll=8)
+            crossing[level, index].wait_recv()
+            lo, hi = spans[index]
+            value = fields[level, STEPS + lo : STEPS + hi] + arrived[level, lo:hi]
+            fields[level, STEPS + lo : STEPS + hi] = value
+            leaving[index, level] = value
+            target, landing = ((before, STEPS + ROWS), (after, 0))[index]
             at = level * index
             copy = remote(
                 leaving.at[index, level, pl.ds(at, STEPS - level)],
@@ -377,12 +395,15 @@
             )
             copy.start()
             halos.append(copy)
-    lax.fori_loop(*spans[2], for_other, 0, unroll=2)
-    crossing.append(core_copies(2))
-    lax.fori_loop(*spans[2], for_own, 0, unroll=2)
-    for copy in crossing[2]:
-        copy.wait_recv()
-    lax.fori_loop(*spans[2], add_arrived, 0)
+    for level in range(2):
+        lax.fori_loop(*spans[2], functools.partial(for_other, level), 0, unroll=4)
+        crossing[level, 2] = cross(level, 2)
+    for level in range(2):
+        lax.fori_loop(*spans[2], functools.partial(for_own, level), 0, unroll=4)
+    for level in range(2):
+        crossing[level, 2].wait_recv()
+        lo, hi = spans[2]
+        fields[level, STEPS + lo : STEPS + hi] = fields[level, STEPS + lo : STEPS + hi] + arrived[level, lo:hi]
     inner_sweeps(fields, speed, middle, beside, False)
     for copy in halos:
         copy.wait_recv()
@@ -396,73 +417,51 @@
 
     edge_sweeps(fields, speed, middle, beside, False)
 
-    results = [
-        pltpu.make_async_copy(fields.at[0, pl.ds(STEPS, ROWS)], s_out.at[own], out_sem.at[0]),
-        remote(fields.at[0, pl.ds(STEPS, ROWS)], s_out.at[own], core_send.at[6], core_recv.at[6], {"shot": away}),
-    ]
-    for copy in results:
-        copy.start()
-
-    def gram_rows(i, total):
+    crossed = remote(
+        fields.at[0, pl.ds(STEPS, ROWS)], sketches.at[own], core_send.at[6], core_recv.at[6], {"shot": away}
+    )
+    crossed.start()
+    kept = pltpu.make_async_copy(fields.at[0, pl.ds(STEPS, ROWS)], sketches.at[own], keep_sem.at[0])
+    kept.start()
+
+    gram = jnp.zeros((2 * RANK, 2 * RANK), F32)
+    for i in range(ROWS // 4):
         value = jnp.concatenate([stacked(fields[0, STEPS + 4 * i + j]) for j in range(4)], 1)
-        return total + dot_rows(value, value)
-
-    gram = lax.fori_loop(0, ROWS // 4, gram_rows, jnp.zeros((2 * RANK, 2 * RANK), F32))
+        gram = gram + dot_rows(value, value)
     gram = gram[:RANK] + gram[RANK:]
     gram = gram[:, :RANK] + gram[:, RANK:]
-    gram = strip_sum(jnp.concatenate([gram, jnp.zeros((RANK, HALF - RANK), F32)], 1), 1)
-    plane_send[2] = gram
-    swap = remote(plane_send.at[2], other_gram, core_send.at[7], core_recv.at[7], {"shot": away})
-    swap.start()
-    swap.wait()
-    theirs = other_gram[...]
-    flag = (own + jnp.zeros((RANK, HALF), jnp.int32)) == 0
-    inv_out[0] = lower_inverse(jnp.where(flag, gram, theirs))
-    inv_out[1] = lower_inverse(jnp.where(flag, theirs, gram))
-
-    for copy in results:
-        copy.wait()
+    packed = jnp.concatenate([gram[:8], gram[8:], jnp.zeros((8, HALF - 2 * RANK), F32)], 1)
+    for side, packed in zip((own, away), gram_sum(packed)):
+        gram = jnp.concatenate([packed, pltpu.roll(packed, HALF - RANK, 1)], 0)
+        high, low = split(lower_inverse(gram) * scale)
+        inverses[side, 0] = high
+        inverses[side, 1] = low
+    crossed.wait_recv()
+    kept.wait()
+    for side, out in enumerate((left_out, right_out)):
+        high, low = (inverses[side, k][:, RANK : 2 * RANK] for k in range(2))
+        lhs = jnp.concatenate([jnp.concatenate([high, high], 1), jnp.concatenate([low, low], 1)], 0)
+
+        def put_block(b, carry):
+            for r in range(STEPS):
+                both = dot(lhs, stacked(sketches[side, b * STEPS + r]))
+                value = both[:RANK] + both[RANK:]
+                for h in range(2):
+                    out.at[b, h].reshape(RANK * STEPS, HALF)[pl.ds(r, RANK, stride=STEPS), :] = (
+                        value[:, h * HALF : (h + 1) * HALF]
+                    )
+            return carry
+
+        lax.fori_loop(0, blocks, put_block, 0)
+
+    crossed.wait_send()
     for copy in edges + halos:
         copy.wait_send()
-    for copies in crossing + list(handed.values()):
+    for copy in crossing.values():
+        copy.wait_send()
+    for copies in handed.values():
         for copy in copies:
             copy.wait_send()
-
-
-def final_kernel(scale, s_hbm, inv_ref, left_out, right_out, sketch, blocks, load_sem, sem):
-    count = ROWS // STEPS
-    loads = {}
-    for b in range(count):
-        for side in range(2):
-            loads[b, side] = pltpu.make_async_copy(
-                s_hbm.at[side, pl.ds(b * STEPS, STEPS)], sketch.at[side, b], load_sem.at[side, b]
-            )
-            loads[b, side].start()
-    lhs = []
-    for side in range(2):
-        high, low = split((inv_ref[side] * scale)[:, RANK : 2 * RANK])
-        lhs.append(jnp.concatenate([jnp.concatenate([high, high], 1), jnp.concatenate([low, low], 1)], 0))
-    copies = []
-    for b in range(count):
-        for side, out in enumerate((left_out, right_out)):
-            loads[b, side].wait()
-            for r in range(STEPS):
-                both = dot(lhs[side], stacked(sketch[side, b, r]))
-                value = both[:RANK] + both[RANK:]
-                for h in range(2):
-                    blocks.at[side, b, h].reshape(RANK * STEPS, HALF)[pl.ds(r, RANK, stride=STEPS), :] = (
-                        value[:, h * HALF : (h + 1) * HALF]
-                    )
-            for h in range(2):
-                copy = pltpu.make_async_copy(
-                    blocks.at[side, b, h],
-                    out.at[:, pl.ds(b * STEPS, STEPS), pl.ds(h * HALF, HALF)],
-                    sem.at[side, b, h],
-                )
-                copy.start()
-                copies.append(copy)
-    for copy in copies:
-        copy.wait()
 
 
 def shards(source_now, source_prev, adjoint_now, adjoint_prev, courant, probe_left, probe_right):
@@ -471,14 +470,12 @@
     vmem_spec = pl.BlockSpec(memory_space=pltpu.VMEM)
     dma = pltpu.SemaphoreType.DMA
     count = ROWS // STEPS
-    sketch, inverse = pl.pallas_call(
-        main_kernel,
-        out_shape=(
-            jax.ShapeDtypeStruct((2, ROWS, RANK, COLS), F32),
-            jax.ShapeDtypeStruct((2, RANK, HALF), F32),
-        ),
+    scale = math.sqrt(ROWS * lax.axis_size("strip") * COLS)
+    factors = pl.pallas_call(
+        functools.partial(main_kernel, scale),
+        out_shape=(pltpu.VMEM((count, 2, RANK, STEPS, HALF), F32),) * 2,
         in_specs=[any_spec] * 7,
-        out_specs=(any_spec, vmem_spec),
+        out_specs=(vmem_spec, vmem_spec),
         scratch_shapes=[
             pltpu.VMEM((4, count, 2, WAVES, STEPS, HALF), F32),
             pltpu.VMEM((4, ROWS, 2 * WAVES, COLS), BF16),
@@ -492,11 +489,16 @@
             pltpu.VMEM((2, TALL, RANK, COLS), F32),
             pltpu.VMEM((2, ROWS, RANK, COLS), F32),
             pltpu.VMEM((2, 2 * RANK, HALF), BF16),
-            pltpu.VMEM((3, RANK, HALF), F32),
-            pltpu.VMEM((2, PLANE - 1, RANK, HALF), F32),
-            pltpu.VMEM((2, RANK, HALF), F32),
-            pltpu.VMEM((2, SIDE - 1, RANK, HALF), F32),
             pltpu.VMEM((RANK, HALF), F32),
+            pltpu.VMEM((PLANE - 1, RANK, HALF), F32),
+            pltpu.VMEM((RANK, HALF), F32),
+            pltpu.VMEM((SIDE - 1, RANK, HALF), F32),
+            pltpu.VMEM((8, HALF), F32),
+            pltpu.VMEM((2, PLANE, 8, HALF), F32),
+            pltpu.VMEM((2, 8, HALF), F32),
+            pltpu.VMEM((SIDE - 1, 2, 8, HALF), F32),
+            pltpu.VMEM((2, ROWS, RANK, COLS), F32),
+            pltpu.VMEM((2, 2, RANK, HALF), BF16),
             pltpu.VMEM((2, TALL, RANK, COLS), F32),
             pltpu.VMEM((2, 2, STEPS, RANK, COLS), F32),
             pltpu.VMEM((2, ROWS, RANK, COLS), F32),
@@ -504,8 +506,8 @@
             dma((1 + 2 * count + 8 * count,)),
             dma((2, 3)),
             dma((2, 3)),
-            dma((2, PLANE + SIDE - 2)),
-            dma((2, PLANE + SIDE - 2)),
+            dma((3 * PLANE + 2 * SIDE - 3,)),
+            dma((3 * PLANE + 2 * SIDE - 3,)),
             dma((8,)),
             dma((8,)),
             dma((2, 2)),
@@ -519,20 +521,7 @@
         ),
         name="sketch",
     )(*waves, courant, probe_left, probe_right)
-    scale = math.sqrt(ROWS * lax.axis_size("strip") * COLS)
-    return pl.pallas_call(
-        functools.partial(final_kernel, scale),
-        out_shape=(jax.ShapeDtypeStruct((RANK, ROWS, COLS), F32),) * 2,
-        in_specs=[any_spec, vmem_spec],
-        out_specs=(any_spec, any_spec),
-        scratch_shapes=[
-            pltpu.VMEM((2, count, STEPS, RANK, COLS), F32),
-            pltpu.VMEM((2, count, 2, RANK, STEPS, HALF), F32),
-            dma((2, count)),
-            dma((2, count, 2)),
-        ],
-        name="factors",
-    )(sketch, inverse)
+    return tuple(factor.transpose(2, 0, 3, 1, 4).reshape(RANK, ROWS, COLS) for factor in factors)
 
 
 def solution(mesh):

time: 62.8 us -> 57.9 us (0.922)
  Pallas kernels: 62 us -> 56 us
  local copies, waits for them, and re-layouts: 0 us -> 1.1 us
    pallas_call x2 -> x1, Pallas kernels: 62 us -> 56 us  [shards(): pl.pallas_call(functools.partial(main_kernel, scale), out_shape=(pltpu.VM...]
    reshape x0 -> x1, local copies, waits for them, and re-layouts: none -> 1.1 us  [shards(): factor.transpose(2, 0, 3, 1, 4).reshape(RANK, ROWS, COLS)]
where the time goes in v3:
time: 57.9 us; the launch traced here: 57.8 us
  Pallas kernels  56 us (97%)
  local copies, waits for them, and re-layouts  1.1 us (2%)
  between operations  0.64 us (1%)
    pallas_call x1, Pallas kernels, shards(): pl.pallas_call(functools.partial(main_kernel, scale), out_shape=(pltpu.VM...  56 us

profile of v3, /device:TPU:1, one launch (start us, length us, event | category | flops | bytes accessed | tf_op | source)
XLA Modules:
  0.0 57.8 jit_solution(11012108129374767772)
XLA Ops:
  0.6 56.0 %sketch.1 = (f32[4,2,16,8,128]{4,3,2,1,0:T(8,128)S(1)}, f32[4,2,16,8,128]{4,3,2,1,0:T(8,128)S(1)}) custom-call(f32[64,32,256]{2,1,0:T(8,128)} %bitcast.14, f32[64,32,256]{2,1,0:T(8,128)} %bitcast.15, f32[64,32,256]{2,1,0:T(8,128)} %bitcast.16, f32[64,32,256]{2,1,0:T(8,128)} %bitcast.17, f32[32,256]{1,0:T(8,128)} %courant.1, f32[16,32,256]{2,1,0:T(8,128)} %probe_left.1, ...), custom_call_target="tpu_custom_call" | custom-call | tf_op jit(solution)/shard_map/sketch/pallas_call | solution.py:474
  56.7 1.1 %copy_bitcast_fusion = (f32[16,32,256]{2,1,0:T(8,128)}, f32[16,32,256]{2,1,0:T(8,128)}) fusion(f32[4,2,16,8,128]{4,3,2,1,0:T(8,128)S(1)} %get-tuple-element.4, f32[4,2,16,8,128]{4,3,2,1,0:T(8,128)S(1)} %get-tuple-element.5), kind=kLoop, calls=%fused_computation | loop fusion | bytes 2097152 | tf_op jit(solution)/shard_map/reshape | solution.py:524

commit v4 on v3

--- a/solution.py
+++ b/solution.py
@@ -97,7 +97,7 @@
     work = jnp.where(lane < RANK, gram, jnp.where(lane == row + RANK, 1.0, 0.0))
     for k in range(RANK):
         pivot = work[k : k + 1, k : k + 1]
-        root = 1.0 / jnp.sqrt(pivot)
+        root = lax.rsqrt(pivot)
         line = work[k : k + 1, :] * root
         column = jnp.where(row[:, :1] > k, work[:, k : k + 1] * root, 0.0)
         work = jnp.where(row == k, line, work - column * line)
@@ -136,7 +136,12 @@
         )
 
     barrier = pltpu.get_barrier_semaphore()
-    strips = [after, before] + [plane_peer(d) for d in FAR_FIRST] + [column_peer(d) for d in COLUMN_FIRST]
+    inside = (me > 0, me < count - 1)
+    for side, peer in enumerate((before, after)):
+        @pl.when(inside[side])
+        def _():
+            pl.semaphore_signal(barrier, inc=1, device_id={"strip": peer}, device_id_type=MESH)
+    strips = [plane_peer(d) for d in FAR_FIRST] + [column_peer(d) for d in COLUMN_FIRST]
     for peer in strips:
         pl.semaphore_signal(barrier, inc=1, device_id={"strip": peer}, device_id_type=MESH)
     pl.semaphore_signal(barrier, inc=1, device_id={"shot": away}, device_id_type=MESH)
@@ -150,11 +155,11 @@
             for h in range(2)
         ]
 
-    def probe_sends(probe):
+    def probe_sends(probe, side):
+        target, first = targets[side]
         return [
             remote(probe.at[:, pl.ds(first, STEPS), halves[h]], probe_edges.at[side, h],
                    edge_send.at[side, 1 + h], edge_recv.at[side, 1 + h], {"strip": target})
-            for side, (target, first) in enumerate(targets)
             for h in range(2)
         ]
 
@@ -181,6 +186,24 @@
         for load in group:
             load.start()
 
+    pl.semaphore_wait(barrier, len(strips) + PLANE + sum(flag.astype(jnp.int32) for flag in inside))
+
+    speed_sends = [
+        remote(courant.at[pl.ds(first, STEPS)], speed_edges.at[side],
+               edge_send.at[side, 0], edge_recv.at[side, 0], {"strip": target})
+        for side, (target, first) in enumerate(targets)
+    ]
+    for side in range(2):
+        @pl.when(inside[1 - side])
+        def _():
+            speed_sends[side].start()
+        for core, probe in enumerate((probe_left, probe_right)):
+            @pl.when(jnp.logical_and(inside[1 - side], own == core))
+            def _():
+                for copy in probe_sends(probe, side):
+                    copy.start()
+    edges = [[speed_sends[side]] + probe_sends(probe_left, side) for side in range(2)]
+
     near = lax.broadcasted_iota(jnp.int32, (COLS, COLS), 0) - lax.broadcasted_iota(jnp.int32, (COLS, COLS), 1)
     beside[...] = jnp.where(jnp.abs(near) == 1, 1.0, 0.0).astype(BF16)
 
@@ -210,22 +233,6 @@
         return carry
 
     lax.fori_loop(0, TALL, put_zero, 0)
-
-    pl.semaphore_wait(barrier, len(strips) + PLANE)
-
-    speed_sends = [
-        remote(courant.at[pl.ds(first, STEPS)], speed_edges.at[side],
-               edge_send.at[side, 0], edge_recv.at[side, 0], {"strip": target})
-        for side, (target, first) in enumerate(targets)
-    ]
-    for copy in speed_sends:
-        copy.start()
-    for core, probe in enumerate((probe_left, probe_right)):
-        @pl.when(own == core)
-        def _():
-            for copy in probe_sends(probe):
-                copy.start()
-    edges = speed_sends + probe_sends(probe_left)
 
     inner_sweeps(steps_p, speed, middle, beside, True)
 
@@ -269,20 +276,21 @@
 
     zero = jnp.zeros((2 * RANK, HALF), F32)
     mine = lax.fori_loop(*spans[2], own_products, zero, unroll=4)
-
-    for copy in edges:
+    for copy in handed[2]:
         copy.wait_recv()
-    inside = (me > 0, me < count - 1)
+    theirs = lax.fori_loop(*spans[2], other_products, zero, unroll=4)
+
     for side, row0 in enumerate((0, STEPS + ROWS)):
+        @pl.when(inside[side])
+        def _():
+            for copy in edges[side]:
+                copy.wait_recv()
         put_speed(jnp.where(inside[side], speed_edges[side], 0.0), row0)
         for r in range(STEPS):
-            steps_p[0, row0 + r] = rows_of(probe_edges, side, r)
+            steps_p[0, row0 + r] = jnp.where(inside[side], rows_of(probe_edges, side, r), 0.0)
     edge_sweeps(steps_p, speed, middle, beside, True)
     for index in range(2):
         handed[index] = hand_over(index)
-    for copy in handed[2]:
-        copy.wait_recv()
-    theirs = lax.fori_loop(*spans[2], other_products, zero, unroll=4)
     for index in range(2):
         mine = lax.fori_loop(*spans[index], own_products, mine, unroll=4)
     for index in range(2):
@@ -377,7 +385,7 @@
         for index in range(2):
             lax.fori_loop(*spans[index], functools.partial(for_other, level), 0, unroll=8)
             crossing[level, index] = cross(level, index)
-    halos = []
+    halos = {}
     for level in range(2):
         for index in range(2):
             lax.fori_loop(*spans[index], functools.partial(for_own, level), 0, unroll=8)
@@ -393,8 +401,8 @@
                 fields.at[level, pl.ds(landing + at, STEPS - level)],
                 halo_send.at[index, level], halo_recv.at[index, level], {"strip": target},
             )
-            copy.start()
-            halos.append(copy)
+            halos[level, index] = copy
+            pl.when(inside[index])(copy.start)
     for level in range(2):
         lax.fori_loop(*spans[2], functools.partial(for_other, level), 0, unroll=4)
         crossing[level, 2] = cross(level, 2)
@@ -405,10 +413,12 @@
         lo, hi = spans[2]
         fields[level, STEPS + lo : STEPS + hi] = fields[level, STEPS + lo : STEPS + hi] + arrived[level, lo:hi]
     inner_sweeps(fields, speed, middle, beside, False)
-    for copy in halos:
-        copy.wait_recv()
-
     for side, row0 in enumerate((0, STEPS + ROWS)):
+        @pl.when(inside[side])
+        def _():
+            for level in range(2):
+                halos[level, 1 - side].wait_recv()
+
         @pl.when(jnp.logical_not(inside[side]))
         def _():
             for level in range(2):
@@ -455,8 +465,14 @@
         lax.fori_loop(0, blocks, put_block, 0)
 
     crossed.wait_send()
-    for copy in edges + halos:
-        copy.wait_send()
+    for side in range(2):
+        @pl.when(inside[side])
+        def _():
+            for copy in edges[1 - side]:
+                copy.wait_send()
+            for level in range(2):
+                halos[level, side].wait_send()
+
     for copy in crossing.values():
         copy.wait_send()
     for copies in handed.values():

time: 57.9 us -> 55.9 us (0.965)
  Pallas kernels: 56 us -> 54.1 us
    pallas_call x1, Pallas kernels: 56 us -> 54.1 us  [shards(): pl.pallas_call(functools.partial(main_kernel, scale), out_shape=(pltpu.VM...]
where the time goes in v4:
time: 55.9 us; the launch traced here: 55.8 us
  Pallas kernels  54.1 us (97%)
  local copies, waits for them, and re-layouts  1.1 us (2%)
  between operations  0.64 us (1%)
    pallas_call x1, Pallas kernels, shards(): pl.pallas_call(functools.partial(main_kernel, scale), out_shape=(pltpu.VM...  54.1 us

profile of v4, /device:TPU:1, one launch (start us, length us, event | category | flops | bytes accessed | tf_op | source)
XLA Modules:
  0.0 55.8 jit_solution(6898305988873468017)
XLA Ops:
  0.6 54.1 %sketch.1 = (f32[4,2,16,8,128]{4,3,2,1,0:T(8,128)S(1)}, f32[4,2,16,8,128]{4,3,2,1,0:T(8,128)S(1)}) custom-call(f32[64,32,256]{2,1,0:T(8,128)} %bitcast.14, f32[64,32,256]{2,1,0:T(8,128)} %bitcast.15, f32[64,32,256]{2,1,0:T(8,128)} %bitcast.16, f32[64,32,256]{2,1,0:T(8,128)} %bitcast.17, f32[32,256]{1,0:T(8,128)} %courant.1, f32[16,32,256]{2,1,0:T(8,128)} %probe_left.1, ...), custom_call_target="tpu_custom_call" | custom-call | tf_op jit(solution)/shard_map/sketch/pallas_call | solution.py:490
  54.7 1.1 %copy_bitcast_fusion = (f32[16,32,256]{2,1,0:T(8,128)}, f32[16,32,256]{2,1,0:T(8,128)}) fusion(f32[4,2,16,8,128]{4,3,2,1,0:T(8,128)S(1)} %get-tuple-element.4, f32[4,2,16,8,128]{4,3,2,1,0:T(8,128)S(1)} %get-tuple-element.5), kind=kLoop, calls=%fused_computation | loop fusion | bytes 2097152 | tf_op jit(solution)/shard_map/reshape | solution.py:540

commit v5 on v4

--- a/solution.py
+++ b/solution.py
@@ -155,10 +155,12 @@
             for h in range(2)
         ]
 
-    def probe_sends(probe, side):
+    def edge_copies(side):
         target, first = targets[side]
-        return [
-            remote(probe.at[:, pl.ds(first, STEPS), halves[h]], probe_edges.at[side, h],
+        speed_copy = remote(speed_own.at[pl.ds(first, STEPS)], speed_edges.at[side],
+                            edge_send.at[side, 0], edge_recv.at[side, 0], {"strip": target})
+        return [speed_copy] + [
+            remote(probes.at[first // STEPS, h], probe_edges.at[side, h],
                    edge_send.at[side, 1 + h], edge_recv.at[side, 1 + h], {"strip": target})
             for h in range(2)
         ]
@@ -186,23 +188,17 @@
         for load in group:
             load.start()
 
+    load_speed.wait()
+    for load in probe_loads(probe_left):
+        load.wait()
     pl.semaphore_wait(barrier, len(strips) + PLANE + sum(flag.astype(jnp.int32) for flag in inside))
 
-    speed_sends = [
-        remote(courant.at[pl.ds(first, STEPS)], speed_edges.at[side],
-               edge_send.at[side, 0], edge_recv.at[side, 0], {"strip": target})
-        for side, (target, first) in enumerate(targets)
-    ]
+    edges = [edge_copies(side) for side in range(2)]
     for side in range(2):
         @pl.when(inside[1 - side])
         def _():
-            speed_sends[side].start()
-        for core, probe in enumerate((probe_left, probe_right)):
-            @pl.when(jnp.logical_and(inside[1 - side], own == core))
-            def _():
-                for copy in probe_sends(probe, side):
-                    copy.start()
-    edges = [[speed_sends[side]] + probe_sends(probe_left, side) for side in range(2)]
+            for copy in edges[side]:
+                copy.start()
 
     near = lax.broadcasted_iota(jnp.int32, (COLS, COLS), 0) - lax.broadcasted_iota(jnp.int32, (COLS, COLS), 1)
     beside[...] = jnp.where(jnp.abs(near) == 1, 1.0, 0.0).astype(BF16)
@@ -213,12 +209,8 @@
             speed[row0 + r] = value
             middle[row0 + r] = 2.0 - 4.0 * value
 
-    load_speed.wait()
     for block in range(blocks):
         put_speed(speed_own[pl.ds(block * STEPS, STEPS), :], STEPS + block * STEPS)
-    for load in probe_loads(probe_left):
-        load.wait()
-
     def rows_of(tiles, b, r):
         return jnp.concatenate([
             tiles.at[b, h].reshape(RANK * STEPS, HALF)[pl.ds(r, RANK, stride=STEPS), :] for h in range(2)
@@ -291,12 +283,14 @@
     edge_sweeps(steps_p, speed, middle, beside, True)
     for index in range(2):
         handed[index] = hand_over(index)
-    for index in range(2):
-        mine = lax.fori_loop(*spans[index], own_products, mine, unroll=4)
+    edge_rows = [r for index in range(2) for r in range(*spans[index])]
+    for r in edge_rows:
+        mine = own_products(r, mine)
     for index in range(2):
         for copy in handed[index]:
             copy.wait_recv()
-        theirs = lax.fori_loop(*spans[index], other_products, theirs, unroll=4)
+    for r in edge_rows:
+        theirs = other_products(r, theirs)
 
     def start(src, dst, k, device):
         copy = remote(src, dst, sum_send.at[k], sum_recv.at[k], device)
@@ -382,13 +376,15 @@
 
     crossing = {}
     for level in range(2):
+        for r in edge_rows:
+            for_other(level, r, 0)
         for index in range(2):
-            lax.fori_loop(*spans[index], functools.partial(for_other, level), 0, unroll=8)
             crossing[level, index] = cross(level, index)
     halos = {}
     for level in range(2):
+        for r in edge_rows:
+            for_own(level, r, 0)
         for index in range(2):
-            lax.fori_loop(*spans[index], functools.partial(for_own, level), 0, unroll=8)
             crossing[level, index].wait_recv()
             lo, hi = spans[index]
             value = fields[level, STEPS + lo : STEPS + hi] + arrived[level, lo:hi]
@@ -413,6 +409,14 @@
         lo, hi = spans[2]
         fields[level, STEPS + lo : STEPS + hi] = fields[level, STEPS + lo : STEPS + hi] + arrived[level, lo:hi]
     inner_sweeps(fields, speed, middle, beside, False)
+
+    def gram_of(i):
+        value = jnp.concatenate([stacked(fields[0, STEPS + 4 * i + j]) for j in range(4)], 1)
+        return dot_rows(value, value)
+
+    gram = jnp.zeros((2 * RANK, 2 * RANK), F32)
+    for i in range(STEPS // 4, (ROWS - STEPS) // 4):
+        gram = gram + gram_of(i)
     for side, row0 in enumerate((0, STEPS + ROWS)):
         @pl.when(inside[side])
         def _():
@@ -434,10 +438,8 @@
     kept = pltpu.make_async_copy(fields.at[0, pl.ds(STEPS, ROWS)], sketches.at[own], keep_sem.at[0])
     kept.start()
 
-    gram = jnp.zeros((2 * RANK, 2 * RANK), F32)
-    for i in range(ROWS // 4):
-        value = jnp.concatenate([stacked(fields[0, STEPS + 4 * i + j]) for j in range(4)], 1)
-        gram = gram + dot_rows(value, value)
+    for i in list(range(STEPS // 4)) + list(range((ROWS - STEPS) // 4, ROWS // 4)):
+        gram = gram + gram_of(i)
     gram = gram[:RANK] + gram[RANK:]
     gram = gram[:, :RANK] + gram[:, RANK:]
     packed = jnp.concatenate([gram[:8], gram[8:], jnp.zeros((8, HALF - 2 * RANK), F32)], 1)
@@ -462,7 +464,7 @@
                     )
             return carry
 
-        lax.fori_loop(0, blocks, put_block, 0)
+        lax.fori_loop(0, blocks, put_block, 0, unroll=blocks)
 
     crossed.wait_send()
     for side in range(2):

time: 55.9 us -> 54.6 us (0.977)
  Pallas kernels: 54.1 us -> 52.8 us
    pallas_call x1, Pallas kernels: 54.1 us -> 52.8 us  [shards(): pl.pallas_call(functools.partial(main_kernel, scale), out_shape=(pltpu.VM...]
where the time goes in v5:
time: 54.6 us; the launch traced here: 54.5 us
  Pallas kernels  52.8 us (97%)
  local copies, waits for them, and re-layouts  1.1 us (2%)
  between operations  0.64 us (1%)
    pallas_call x1, Pallas kernels, shards(): pl.pallas_call(functools.partial(main_kernel, scale), out_shape=(pltpu.VM...  52.8 us
    reshape x1, local copies, waits for them, and re-layouts, shards(): factor.transpose(2, 0, 3, 1, 4).reshape(RANK, ROWS, COLS)  1.1 us

profile of v5, /device:TPU:1, one launch (start us, length us, event | category | flops | bytes accessed | tf_op | source)
XLA Modules:
  0.0 54.5 jit_solution(3658273744501252957)
XLA Ops:
  0.6 52.8 %sketch.1 = (f32[4,2,16,8,128]{4,3,2,1,0:T(8,128)S(1)}, f32[4,2,16,8,128]{4,3,2,1,0:T(8,128)S(1)}) custom-call(f32[64,32,256]{2,1,0:T(8,128)} %bitcast.14, f32[64,32,256]{2,1,0:T(8,128)} %bitcast.15, f32[64,32,256]{2,1,0:T(8,128)} %bitcast.16, f32[64,32,256]{2,1,0:T(8,128)} %bitcast.17, f32[32,256]{1,0:T(8,128)} %courant.1, f32[16,32,256]{2,1,0:T(8,128)} %probe_left.1, ...), custom_call_target="tpu_custom_call" | custom-call | tf_op jit(solution)/shard_map/sketch/pallas_call | solution.py:492
  53.4 1.1 %copy_bitcast_fusion = (f32[16,32,256]{2,1,0:T(8,128)}, f32[16,32,256]{2,1,0:T(8,128)}) fusion(f32[4,2,16,8,128]{4,3,2,1,0:T(8,128)S(1)} %get-tuple-element.4, f32[4,2,16,8,128]{4,3,2,1,0:T(8,128)S(1)} %get-tuple-element.5), kind=kLoop, calls=%fused_computation | loop fusion | bytes 2097152 | tf_op jit(solution)/shard_map/reshape | solution.py:542

commit v6 on v5

--- a/solution.py
+++ b/solution.py
@@ -59,8 +59,7 @@
 
 
 def advance(buf, speed, middle, beside, level, starts, count, transposed):
-    now = buf.at[lax.rem(level + 1, 2)]
-    new = buf.at[lax.rem(level, 2)]
+    now, new = buf.at[(level + 1) % 2], buf.at[level % 2]
     pieces = []
     for low in starts:
         cells = load_rows(now, low - 1, count + 2)
@@ -88,7 +87,8 @@
         advance(buf, speed, middle, beside, level, (level, STEPS + ROWS - level), STEPS, transposed)
         return carry
 
-    lax.fori_loop(1, STEPS + 1, body, 0)
+    for level in range(1, STEPS + 1):
+        body(level, 0)
 
 
 def lower_inverse(gram):

time: 54.6 us -> 54 us (0.989)
  Pallas kernels: 52.8 us -> 52.1 us
    pallas_call x1, Pallas kernels: 52.8 us -> 52.1 us  [shards(): pl.pallas_call(functools.partial(main_kernel, scale), out_shape=(pltpu.VM...]
where the time goes in v6:
time: 54 us; the launch traced here: 53.9 us
  Pallas kernels  52.1 us (96%)
  local copies, waits for them, and re-layouts  1.1 us (2%)
  between operations  0.64 us (1%)
    pallas_call x1, Pallas kernels, shards(): pl.pallas_call(functools.partial(main_kernel, scale), out_shape=(pltpu.VM...  52.1 us
    reshape x1, local copies, waits for them, and re-layouts, shards(): factor.transpose(2, 0, 3, 1, 4).reshape(RANK, ROWS, COLS)  1.1 us

profile of v6, /device:TPU:1, one launch (start us, length us, event | category | flops | bytes accessed | tf_op | source)
XLA Modules:
  0.0 53.9 jit_solution(14966243925551541295)
XLA Ops:
  0.6 52.1 %sketch.1 = (f32[4,2,16,8,128]{4,3,2,1,0:T(8,128)S(1)}, f32[4,2,16,8,128]{4,3,2,1,0:T(8,128)S(1)}) custom-call(f32[64,32,256]{2,1,0:T(8,128)} %bitcast.14, f32[64,32,256]{2,1,0:T(8,128)} %bitcast.15, f32[64,32,256]{2,1,0:T(8,128)} %bitcast.16, f32[64,32,256]{2,1,0:T(8,128)} %bitcast.17, f32[32,256]{1,0:T(8,128)} %courant.1, f32[16,32,256]{2,1,0:T(8,128)} %probe_left.1, ...), custom_call_target="tpu_custom_call" | custom-call | tf_op jit(solution)/shard_map/sketch/pallas_call | solution.py:492
  52.8 1.1 %copy_bitcast_fusion = (f32[16,32,256]{2,1,0:T(8,128)}, f32[16,32,256]{2,1,0:T(8,128)}) fusion(f32[4,2,16,8,128]{4,3,2,1,0:T(8,128)S(1)} %get-tuple-element.4, f32[4,2,16,8,128]{4,3,2,1,0:T(8,128)S(1)} %get-tuple-element.5), kind=kLoop, calls=%fused_computation | loop fusion | bytes 2097152 | tf_op jit(solution)/shard_map/reshape | solution.py:542
